TPU v7x, 512 devices: a whole 4x4x16 slice. The times are simulated.
512 devices in a mesh: stops: 256 (over y, x, z), veh: 2 (over core).
Axes of the slice: x: 4, y: 4, z: 16, core: 2. Of those that a mesh axis runs over, the one named last changes fastest.
Arguments:
- customer_features: bfloat16 [1048576, 128], P('stops'), may hold values from -20 to 20, as said below
- customer_loads: int32 [1048576], P('stops'), may hold values from 1 to 8
- truck_limits: int32 [2048], replicated, may hold values from 1536 to 3072
- truck_features: bfloat16 [2048, 128], replicated, may hold values from -20 to 20
- customer_average_matrix: bfloat16 [128, 128], replicated, may hold values from -1.5 to 1.5
- truck_identity_matrix: bfloat16 [128, 128], replicated, may hold values from -0.5 to 0.5
- hidden_offset: float32 [128], replicated, may hold values from -4 to 4
- output_projector: bfloat16 [128, 128], replicated, may hold values from -0.5 to 0.5
Outputs:
- new_vehicles: bfloat16 [2048, 128], P('veh')
Inputs may be any that keep to these rules, and one draw needn't show every extreme that they name: `customer_features`: stop embeddings; stops of one block of 4096 form one region.
All inputs are finite; a program needn't handle non-finite values.
Results may differ from a plain program's by a relative error of at most 0.0085.
Values may be sent and summed in bfloat16 or wider, within the bound.
No kernel may reach another device: no remote copies, remote signals or barrier semaphores. Data moves between devices by JAX's collectives and lax.ppermute only.
A program may use at most 64 MiB of HBM per device.

v0:
```python
import jax
import jax.numpy as jnp
from jax import lax
from jax.sharding import PartitionSpec as P


def joined(part, axis, combine):
    gathered = jax.tree.map(lambda a: lax.all_gather(a, axis), part)

    def take(source):
        return jax.tree.map(lambda a: lax.dynamic_index_in_dim(a, source, 0, False), gathered)

    return lax.fori_loop(
        1, lax.axis_size(axis), lambda source, state: combine(state, take(source)), take(0)
    )


def join_parts(first, second):
    top = jnp.maximum(first[0], second[0])
    total = first[1] * jnp.exp(first[0] - top) + second[1] * jnp.exp(second[0] - top)
    return (top, total)


def row_lse(values):
    top = jnp.max(values, axis=1)
    total = jnp.sum(jnp.exp(values - top[:, None]), axis=1)
    top, total = joined((top, total), "veh", join_parts)
    return top + jnp.log(total)


def update_rows(
    num,
    den,
    own_rows,
    customer_average_matrix,
    truck_identity_matrix,
    hidden_offset,
    output_projector,
):
    centroid = (num / den[:, None]).astype(jnp.bfloat16)
    pre = jnp.dot(centroid, customer_average_matrix, preferred_element_type=jnp.float32)
    pre = (
        pre
        + jnp.dot(own_rows, truck_identity_matrix, preferred_element_type=jnp.float32)
        + hidden_offset[None, :]
    )
    hidden = jax.nn.silu(pre).astype(jnp.bfloat16)
    update = jnp.dot(hidden, output_projector, preferred_element_type=jnp.float32)
    return (own_rows.astype(jnp.float32) + update).astype(jnp.bfloat16)


def on_device(
    customer_features,
    customer_loads,
    truck_limits,
    truck_features,
    customer_average_matrix,
    truck_identity_matrix,
    hidden_offset,
    output_projector,
):
    width = truck_features.shape[1]
    scale = 1.0 / width**0.5
    veh_count = lax.axis_size("veh")
    truck_index = lax.axis_index("veh")
    radius_span = truck_features.shape[0] // veh_count
    my_veh = lax.dynamic_slice_in_dim(truck_features, truck_index * radius_span, radius_span, 0)
    local_capacity = lax.dynamic_slice_in_dim(
        truck_limits, truck_index * radius_span, radius_span, 0
    )
    log_a = jnp.log(customer_loads.astype(jnp.float32))
    target_share_logarithm = jnp.log(local_capacity.astype(jnp.float32))
    scores = jnp.dot(customer_features, my_veh.T, preferred_element_type=jnp.float32) * scale
    f_one = log_a - row_lse(scores)
    col_part = jnp.sum(jnp.exp(f_one[:, None] + scores), axis=0)
    colsum = lax.psum(col_part, "stops")
    g_one = target_share_logarithm - jnp.log(colsum)
    f_two = log_a - row_lse(scores + g_one[None, :])
    plan = jnp.exp(f_two[:, None] + g_one[None, :] + scores).astype(jnp.bfloat16)
    den = jnp.sum(plan, axis=0, dtype=jnp.float32)
    num = lax.dot_general(
        plan, customer_features, (((0,), (0,)), ((), ())), preferred_element_type=jnp.float32
    )
    num, den = lax.psum((num, den), "stops")
    return update_rows(
        num,
        den,
        my_veh,
        customer_average_matrix,
        truck_identity_matrix,
        hidden_offset,
        output_projector,
    )


def solution(mesh):
    placed = (P("stops", None), P("stops"), P(), P(), P(), P(), P(), P())
    return jax.shard_map(
        on_device, mesh=mesh, in_specs=placed, out_specs=P("veh", None), check_vma=False
    )
```

profile of v0, /device:TPU:32, one launch (start us, length us, event | category | flops | bytes accessed | tf_op | source)
XLA Modules:
  0.0 1458.4 jit_solution(17495390267495161967)
XLA Ops:
  6.5 1.2 copy-done
  7.8 9.0 multiply_reduce_fusion
  16.8 1.8 all-gather
  18.6 8.5 fusion.1
  27.1 1.8 all-gather.1
  29.0 0.0 copy-done.2
  29.0 8.6 fusion.3
  37.6 690.8 %psum.21 = f32[1024]{0:T(1024)S(1)} all-reduce(f32[1024]{0:T(1024)S(1)} %fusion.3), channel_id=1, replica_groups=mesh['stops'=256,'veh'=2] {'stops'}, use_global_device_ids=true, to_apply=%region_3.4 | all-reduce | flops 1024 | bytes 8192 | tf_op jit(solution)/shard_map/psum | solution.py:76
  728.5 7.7 fusion.6
  736.2 7.8 exponential_reduce_fusion
  744.0 1.8 all-gather.2
  745.8 2.0 all-gather.3
  747.9 0.0 copy-start.4
  747.9 0.0 copy-start.1
  747.9 0.0 copy-start.5
  747.9 0.0 copy-start.6
  747.9 0.0 copy-start.7
  747.9 8.5 convert_reduce_fusion
  756.4 3.1 fusion.31
  759.5 0.0 all-reduce.2.cloned.1.call-update
  759.5 689.5 %psum.23 = f32[1024]{0:T(1024)S(1)} all-reduce(f32[1024]{0:T(1024)S(1)} %get-tuple-element.27), channel_id=1, replica_groups=mesh['stops'=256,'veh'=2] {'stops'}, use_global_device_ids=true, to_apply=%region_8.9 | all-reduce | flops 1024 | bytes 8192 | tf_op jit(solution)/shard_map/psum | solution.py:84
  1449.0 0.0 all-reduce.2.cloned.1.call-done
  1449.0 1.4 fusion.11
  1450.4 1.1 fusion.8
  (13 shorter events, 0.1 us)
Async XLA Ops:
  6.5 1.2 copy-start
  6.5 1442.5 %all-reduce.2.cloned.1.call-start = ((), (), s32[]{:S(2)}) async-start(), calls=%async_computation | async-start | bytes 1048576 | tf_op jit(solution)/shard_map/psum | solution.py:84
  7.8 21.2 %copy-start.2 = (s32[4096]{0:T(1024)S(1)}, s32[4096]{0:T(1024)}, u32[]{:S(2)}) copy-start(s32[4096]{0:T(1024)} %param.9) | copy-start | bytes 49156
  18.6 709.8 %copy-start.3 = (s32[2048]{0:T(1024)S(1)}, s32[2048]{0:T(1024)}, u32[]{:S(2)}) copy-start(s32[2048]{0:T(1024)} %param.10) | copy-start | bytes 24580
  747.9 701.2 %copy-start.4 = (bf16[128,128]{1,0:T(8,128)(2,1)S(1)}, bf16[128,128]{1,0:T(8,128)(2,1)}, u32[]{:S(2)}) copy-start(bf16[128,128]{1,0:T(8,128)(2,1)} %param.12) | copy-start | bytes 98308
  747.9 702.5 %copy-start.1 = (bf16[2048,128]{1,0:T(8,128)(2,1)S(1)}, bf16[2048,128]{1,0:T(8,128)(2,1)}, u32[]{:S(2)}) copy-start(bf16[2048,128]{1,0:T(8,128)(2,1)} %param.11) | copy-start | bytes 1572868
  747.9 702.5 %copy-start.5 = (bf16[128,128]{1,0:T(8,128)(2,1)S(1)}, bf16[128,128]{1,0:T(8,128)(2,1)}, u32[]{:S(2)}) copy-start(bf16[128,128]{1,0:T(8,128)(2,1)} %param.15) | copy-start | bytes 98308
  747.9 702.5 %copy-start.6 = (bf16[128,128]{1,0:T(8,128)(2,1)S(1)}, bf16[128,128]{1,0:T(8,128)(2,1)}, u32[]{:S(2)}) copy-start(bf16[128,128]{1,0:T(8,128)(2,1)} %param.13) | copy-start | bytes 98308
  747.9 702.5 %copy-start.7 = (f32[128]{0:T(128)S(1)}, f32[128]{0:T(128)}, u32[]{:S(2)}) copy-start(f32[128]{0:T(128)} %param.14) | copy-start | bytes 1540
Sparse Core Ops, SparseCore 0:
  759.7 383.6 all-reduce.1
where the time goes:
time: 1460 us
  blocking collectives  1390 us (95%)
  other arithmetic  41.2 us (3%)
  matrix products  14.6 us (1%)
    psum x1, blocking collectives, on_device(): colsum = lax.psum(col_part, 'stops')  691 us
    psum x1, blocking collectives, on_device(): num, den = lax.psum((num, den), 'stops')  689 us
  transfers between devices with their start and end apart: 1, of which 0 were waited for; matrix products, arithmetic and copies ran while one was open for 0% of the time, Pallas kernels for 0%

commit v1 on v0

v1 whole, which is shorter than its diff:
```python
import jax
import jax.numpy as jnp
from jax import lax
from jax.experimental import pallas as pl
from jax.experimental.pallas import tpu as pltpu
from jax.sharding import Mesh, PartitionSpec as P

F32 = jnp.float32
BF16 = jnp.bfloat16
LANES = 128
BLOCK = 256
CHUNK = 256
LOG2E = 1.4426950408889634
ROW_BITS = 90.0
CAP_SCALE = 2.0**-20
WEIGHT_SCALE = 2.0**50


def on_lanes(column):
    n = column.shape[0] // LANES
    tiles = column.reshape(n, LANES, LANES)
    shape = (n, LANES, LANES)
    eye = lax.broadcasted_iota(jnp.int32, shape, 1) == lax.broadcasted_iota(jnp.int32, shape, 2)
    return jnp.sum(jnp.where(eye, tiles, 0.0), axis=1)


def row_of(ref, first, width):
    return jnp.concatenate(
        [ref[pl.ds(first + i, 1), :] for i in range(width // LANES)], axis=1
    )


def first_kernel(half_ref, veh_ref, stop_ref, load_ref, e_ref, out_ref, z_ref, col_ref):
    step = pl.program_id(0)
    vehicles, width = veh_ref.shape
    scale = LOG2E / width**0.5

    @pl.when(step == 0)
    def _():
        col_ref[...] = jnp.zeros_like(col_ref)

    stops = stop_ref[...]
    top = jnp.full((8, BLOCK), -jnp.inf, F32)
    for c in range(vehicles // CHUNK):
        rows = pl.ds(c * CHUNK, CHUNK)
        z = lax.dot_general(
            veh_ref[rows, :], stops, (((1,), (1,)), ((), ())), preferred_element_type=F32
        )
        z_ref[rows, :] = z
        top = jnp.maximum(top, jnp.max(z.reshape(CHUNK // 8, 8, BLOCK), axis=0))
    top = jnp.max(top, axis=0, keepdims=True) - ROW_BITS / scale
    total = jnp.zeros((8, BLOCK), F32)
    for c in range(vehicles // CHUNK):
        rows = pl.ds(c * CHUNK, CHUNK)
        e = jnp.exp2((z_ref[rows, :] - top) * scale)
        total = total + jnp.sum(e.reshape(CHUNK // 8, 8, BLOCK), axis=0)
        e_ref[0, rows, :] = e.astype(BF16)
    total = jnp.sum(total, axis=0, keepdims=True)
    first = half_ref[0] * (load_ref.shape[0] // 2) + step * (BLOCK // LANES)
    loads = row_of(load_ref, first, BLOCK).astype(F32)
    share = jnp.broadcast_to((loads / total).astype(BF16), (LANES, BLOCK))
    for c in range(vehicles // CHUNK):
        rows = pl.ds(c * CHUNK, CHUNK)
        col_ref[rows, :] += lax.dot_general(
            e_ref[0, rows, :], share, (((1,), (1,)), ((), ())), preferred_element_type=F32
        )

    @pl.when(step == pl.num_programs(0) - 1)
    def _():
        col = on_lanes(col_ref[...]).astype(BF16)
        out_ref[...] = jnp.broadcast_to(col[None], out_ref.shape)


def first_pass(half, veh, stops, loads, peers):
    vehicles, width = veh.shape
    blocks = stops.shape[0] // 2 // BLOCK
    return pl.pallas_call(
        first_kernel,
        grid_spec=pltpu.PrefetchScalarGridSpec(
            num_scalar_prefetch=1,
            grid=(blocks,),
            in_specs=[
                pl.BlockSpec((vehicles, width), lambda s, h: (0, 0)),
                pl.BlockSpec((BLOCK, width), lambda s, h: (h[0] * blocks + s, 0)),
                pl.BlockSpec(loads.shape, lambda s, h: (0, 0)),
            ],
            out_specs=[
                pl.BlockSpec((1, vehicles, BLOCK), lambda s, h: (s, 0, 0)),
                pl.BlockSpec((peers, vehicles // LANES, LANES), lambda s, h: (0, 0, 0)),
            ],
            scratch_shapes=[
                pltpu.VMEM((vehicles, BLOCK), F32),
                pltpu.VMEM((vehicles, LANES), F32),
            ],
        ),
        out_shape=[
            jax.ShapeDtypeStruct((blocks, vehicles, BLOCK), BF16),
            jax.ShapeDtypeStruct((peers, vehicles // LANES, LANES), BF16),
        ],
        compiler_params=pltpu.CompilerParams(vmem_limit_bytes=32 << 20),
        name="first_pass",
    )(half, veh, stops, loads)


def sum_and_copy_kernel(in_ref, out_ref):
    total = jnp.sum(in_ref[...].astype(F32), axis=0)
    out_ref[...] = jnp.broadcast_to(total.astype(out_ref.dtype)[None], out_ref.shape)


def sum_and_copy(parts, copies):
    return pl.pallas_call(
        sum_and_copy_kernel,
        out_shape=jax.ShapeDtypeStruct((copies,) + parts.shape[1:], parts.dtype),
        name="sum_and_copy",
    )(parts)


def second_kernel(half_ref, cap_ref, part_ref, load_ref, stop_ref, e_ref, out_ref, g_ref, num_ref):
    step = pl.program_id(0)
    vehicles = num_ref.shape[0]

    @pl.when(step == 0)
    def _():
        num_ref[...] = jnp.zeros_like(num_ref)
        colsum = jnp.sum(part_ref[...].astype(F32), axis=0)
        g = (cap_ref[...].astype(F32) * CAP_SCALE) / colsum
        shape = (LANES, LANES)
        eye = lax.broadcasted_iota(jnp.int32, shape, 0) == lax.broadcasted_iota(jnp.int32, shape, 1)
        for r in range(vehicles // LANES):
            spread = jnp.where(eye, jnp.broadcast_to(g[r : r + 1], shape), 0.0)
            column = jnp.sum(spread, axis=1, keepdims=True)
            g_ref[pl.ds(r * LANES, LANES), :] = jnp.broadcast_to(column, shape)

    total = jnp.zeros((8, BLOCK), F32)
    for c in range(vehicles // CHUNK):
        rows = pl.ds(c * CHUNK, CHUNK)
        g = g_ref[rows, :]
        t = e_ref[0, rows, :].astype(F32) * jnp.concatenate([g] * (BLOCK // LANES), axis=1)
        total = total + jnp.sum(t.reshape(CHUNK // 8, 8, BLOCK), axis=0)
    total = jnp.sum(total, axis=0, keepdims=True)
    first = half_ref[0] * (load_ref.shape[0] // 2) + step * (BLOCK // LANES)
    loads = row_of(load_ref, first, BLOCK).astype(F32)
    weight = (loads * WEIGHT_SCALE / total).astype(BF16).astype(F32)
    scaled = stop_ref[...].astype(F32).T * weight
    right = jnp.concatenate(
        [scaled.astype(BF16), jnp.broadcast_to(weight.astype(BF16), (LANES, BLOCK))], axis=0
    )
    for c in range(vehicles // CHUNK):
        rows = pl.ds(c * CHUNK, CHUNK)
        num_ref[rows, :] += lax.dot_general(
            e_ref[0, rows, :], right, (((1,), (1,)), ((), ())), preferred_element_type=F32
        )

    @pl.when(step == pl.num_programs(0) - 1)
    def _():
        peers, tall, width = out_ref.shape
        own = vehicles // peers
        half = peers // 2
        shape = (own, LANES)
        eye = lax.broadcasted_iota(jnp.int32, shape, 0) == lax.broadcasted_iota(jnp.int32, shape, 1)
        line = lax.broadcasted_iota(jnp.int32, (tall - own, LANES), 0)
        for v in range(2):
            for r in range(half):
                rows = pl.ds((v * half + r) * own, own)
                out_ref[r * 2 + v, 0:own, :] = num_ref[rows, 0:width].astype(BF16)
                den = jnp.sum(jnp.where(eye, num_ref[rows, width:], 0.0), axis=0, keepdims=True)
                high = den.astype(BF16).astype(F32)
                tail = jnp.where(line == 0, high, jnp.where(line == 1, den - high, 0.0))
                out_ref[r * 2 + v, own:tall, :] = tail.astype(BF16)


def second_pass(half, caps, parts, loads, stops, e, peers):
    blocks, vehicles, _ = e.shape
    width = stops.shape[1]
    tall = vehicles // peers + 8
    return pl.pallas_call(
        second_kernel,
        grid_spec=pltpu.PrefetchScalarGridSpec(
            num_scalar_prefetch=1,
            grid=(blocks,),
            in_specs=[
                pl.BlockSpec(caps.shape, lambda s, h: (0, 0)),
                pl.BlockSpec(parts.shape, lambda s, h: (0, 0, 0)),
                pl.BlockSpec(loads.shape, lambda s, h: (0, 0)),
                pl.BlockSpec((BLOCK, width), lambda s, h: (h[0] * blocks + s, 0)),
                pl.BlockSpec((1, vehicles, BLOCK), lambda s, h: (s, 0, 0)),
            ],
            out_specs=pl.BlockSpec((peers, tall, width), lambda s, h: (0, 0, 0)),
            scratch_shapes=[
                pltpu.VMEM((vehicles, LANES), F32),
                pltpu.VMEM((vehicles, width + LANES), F32),
            ],
        ),
        out_shape=jax.ShapeDtypeStruct((peers, tall, width), BF16),
        compiler_params=pltpu.CompilerParams(vmem_limit_bytes=32 << 20),
        name="second_pass",
    )(half, caps, parts, loads, stops, e)


def update_kernel(
    where_ref, part_ref, veh_ref, average_ref, identity_ref, offset_ref, projector_ref, out_ref
):
    own, width = veh_ref.shape
    total = jnp.sum(part_ref[...].astype(F32), axis=0)
    den = total[own : own + 1, :] + total[own + 1 : own + 2, :]
    shape = (own, LANES)
    eye = lax.broadcasted_iota(jnp.int32, shape, 0) == lax.broadcasted_iota(jnp.int32, shape, 1)
    den = jnp.sum(jnp.where(eye, jnp.broadcast_to(den, shape), 0.0), axis=1, keepdims=True)
    centroid = (total[0:own] / den).astype(BF16)
    rows = veh_ref[...]
    pre = jnp.dot(centroid, average_ref[...], preferred_element_type=F32)
    pre = pre + jnp.dot(rows, identity_ref[...], preferred_element_type=F32) + offset_ref[...]
    hidden = jax.nn.silu(pre).astype(BF16)
    update = jnp.dot(hidden, projector_ref[...], preferred_element_type=F32)
    new = (rows.astype(F32) + update).astype(BF16)
    out_ref[...] = jnp.broadcast_to(new[None], out_ref.shape)


def update_rows(where, parts, veh, average, identity, offset, projector, copies, own):
    width = veh.shape[1]
    whole = lambda s, w: (0, 0)
    return pl.pallas_call(
        update_kernel,
        grid_spec=pltpu.PrefetchScalarGridSpec(
            num_scalar_prefetch=1,
            grid=(1,),
            in_specs=[
                pl.BlockSpec(parts.shape, lambda s, w: (0, 0, 0)),
                pl.BlockSpec((own, width), lambda s, w: (w[0], 0)),
                pl.BlockSpec(average.shape, whole),
                pl.BlockSpec(identity.shape, whole),
                pl.BlockSpec(offset.shape, whole),
                pl.BlockSpec(projector.shape, whole),
            ],
            out_specs=pl.BlockSpec((copies, own, width), lambda s, w: (0, 0, 0)),
        ),
        out_shape=jax.ShapeDtypeStruct((copies, own, width), BF16),
        name="update_rows",
    )(where, parts, veh, average, identity, offset, projector)


def swap(array, axes):
    return lax.all_to_all(array, axes, 0, 0, tiled=True)


def solution(mesh):
    stops_n = mesh.shape["stops"]
    y = x = 4
    pair = 2
    far = stops_n // (y * x * pair)
    inner = Mesh(
        mesh.devices.reshape(y, x, far, pair, mesh.shape["veh"]), ("y", "x", "far", "pair", "veh")
    )

    def on_device(
        customer_features,
        customer_loads,
        truck_limits,
        truck_features,
        customer_average_matrix,
        truck_identity_matrix,
        hidden_offset,
        output_projector,
    ):
        vehicles, width = truck_features.shape
        core = lax.axis_index("veh")
        half = core.astype(jnp.int32).reshape(1)
        near = (lax.axis_index("y") * x + lax.axis_index("x")) * pair + lax.axis_index("pair")
        chips = y * x * pair
        where = (core * chips + near).astype(jnp.int32).reshape(1)
        loads = customer_loads.reshape(-1, LANES)
        caps = truck_limits.reshape(-1, LANES)

        e, col = first_pass(half, truck_features, customer_features, loads, y * x * 2)
        col = swap(col, ("y", "x", "veh"))
        col = swap(sum_and_copy(col, far * pair), ("far", "pair"))
        parts = second_pass(half, caps, col, loads, customer_features, e, chips * 2)
        parts = swap(parts, ("y", "x", "pair", "veh"))
        parts = swap(sum_and_copy(parts, far), "far")
        new = update_rows(
            where,
            parts,
            truck_features,
            customer_average_matrix,
            truck_identity_matrix,
            hidden_offset.reshape(1, -1),
            output_projector,
            chips,
            vehicles // (chips * 2),
        )
        new = swap(new, ("y", "x", "pair"))
        return new.reshape(-1, width)

    split = ("y", "x", "far", "pair")
    placed = (P(split, None), P(split), P(), P(), P(), P(), P(), P())
    return jax.shard_map(
        on_device, mesh=inner, in_specs=placed, out_specs=P("veh", None), check_vma=False
    )
```

time: 1460 us -> 129 us (0.09)
  the two profiles are of different devices: /device:TPU:32 before, /device:TPU:2 now
where the time goes in v1:
time: 129 us; the launch traced here: 128 us
  blocking collectives  75.1 us (58%)
  Pallas kernels  22.8 us (18%)
  local copies, waits for them, and re-layouts  13.5 us (10%)
  waiting for transfers between devices  13.5 us (10%)
  starting transfers between devices  3.36 us (3%)
    all_to_all x4, blocking collectives, swap(): return lax.all_to_all(array, axes, 0, 0, tiled=True)  75.1 us
    unnamed x19, local copies, waits for them, and re-layouts  13.5 us
    all_to_all x1, waiting for transfers between devices, swap(): return lax.all_to_all(array, axes, 0, 0, tiled=True)  13.5 us
    pallas_call x1, Pallas kernels, first_pass(): pl.pallas_call(first_kernel, grid_spec=pltpu.PrefetchScalarGridSpec(num_s...  11.1 us
    pallas_call x1, Pallas kernels, second_pass(): pl.pallas_call(second_kernel, grid_spec=pltpu.PrefetchScalarGridSpec(num_...  6.4 us
    pallas_call x2, Pallas kernels, sum_and_copy(): pl.pallas_call(sum_and_copy_kernel, out_shape=jax.ShapeDtypeStruct((copie...  3.41 us
    all_to_all x1, starting transfers between devices, swap(): return lax.all_to_all(array, axes, 0, 0, tiled=True)  3.36 us
  transfers between devices with their start and end apart: 1, of which 1 were waited for; matrix products, arithmetic and copies ran while one was open for 0% of the time, Pallas kernels for 0%

profile of v1, /device:TPU:2, one launch (start us, length us, event | category | flops | bytes accessed | tf_op | source)
XLA Modules:
  0.0 128.4 jit_solution(13186852622201617855)
XLA Ops:
  0.0 0.0 copy-start.2
  0.0 1.2 copy-done.2
  1.2 0.0 copy-start.4
  1.2 1.0 copy-done.4
  2.3 0.7 copy-done.5
  3.0 11.1 %first_pass.1 = (bf16[8,2048,256]{2,1,0:T(8,128)(2,1)S(1)}, bf16[32,16,128]{2,1,0:T(8,128)(2,1)S(1)}) custom-call(s32[1]{0:T(128)} %bitcast.1.half_ref, bf16[2048,128]{1,0:T(8,128)(2,1)S(1)} %copy-done.4, bf16[4096,128]{1,0:T(8,128)(2,1)S(1)} %copy-done.2, s32[32,128]{1,0:T(8,128)S(1)} %bitcast.6), custom_call_target="tpu_custom_call" | custom-call | tf_op jit(solution)/shard_map/first_pass/pallas_call | solution.py:77
  14.0 0.0 copy-start
  14.1 3.2 %copy-done = bf16[8,2048,256]{2,1,0:T(8,128)(2,1)} copy-done((bf16[8,2048,256]{2,1,0:T(8,128)(2,1)}, bf16[8,2048,256]{2,1,0:T(8,128)(2,1)S(1)}, u32[]{:S(2)}) %copy-start) | copy-done | bytes 8388632
  17.3 15.9 %all_to_all.25.in_ref = bf16[32,16,128]{2,1,0:T(8,128)(2,1)} all-to-all(bf16[32,16,128]{2,1,0:T(8,128)(2,1)S(1)} %get-tuple-element.7), channel_id=1, replica_groups=mesh['y'=4,'x'=4,'far'=8,'pair'=2,'veh'=2] {'y','x','veh'}, dimensions={0} | all-to-all | bytes 262144 | tf_op jit(solution)/shard_map/all_to_all | solution.py:243
  33.2 1.6 %sum_and_copy.2 = bf16[16,16,128]{2,1,0:T(8,128)(2,1)} custom-call(bf16[32,16,128]{2,1,0:T(8,128)(2,1)} %all_to_all.25.in_ref), custom_call_target="tpu_custom_call" | custom-call | tf_op jit(solution)/shard_map/sum_and_copy/pallas_call | solution.py:111
  34.8 26.5 %all_to_all.26.part_ref = bf16[16,16,128]{2,1,0:T(8,128)(2,1)S(1)} all-to-all(bf16[16,16,128]{2,1,0:T(8,128)(2,1)} %sum_and_copy.2), channel_id=1, replica_groups=mesh['y'=4,'x'=4,'far'=8,'pair'=2,'veh'=2] {'far','pair'}, dimensions={0} | all-to-all | bytes 131072 | tf_op jit(solution)/shard_map/all_to_all | solution.py:243
  61.3 3.4 %copy-done.1 = bf16[8,2048,256]{2,1,0:T(8,128)(2,1)S(1)} copy-done((bf16[8,2048,256]{2,1,0:T(8,128)(2,1)S(1)}, bf16[8,2048,256]{2,1,0:T(8,128)(2,1)}, u32[]{:S(2)}) %copy-start.1) | copy-done | bytes 8388632
  64.6 1.2 copy-done.3
  65.9 0.7 copy-done.6
  66.6 0.7 copy-done.7
  67.3 6.4 %second_pass.1 = bf16[64,40,128]{2,1,0:T(8,128)(2,1)S(1)} custom-call(s32[1]{0:T(128)} %bitcast.1.half_ref, s32[16,128]{1,0:T(8,128)S(1)} %bitcast.8, bf16[16,16,128]{2,1,0:T(8,128)(2,1)S(1)} %all_to_all.26.part_ref, s32[32,128]{1,0:T(8,128)S(1)} %bitcast.7, bf16[4096,128]{1,0:T(8,128)(2,1)S(1)} %copy-done.3, bf16[8,2048,256]{2,1,0:T(8,128)(2,1)S(1)} %copy-done.1), custom_call_target="tpu_custom_call" | custom-call | tf_op jit(solution)/shard_map/second_pass/pallas_call | solution.py:176
  73.7 18.5 %all_to_all.27.in_ref = bf16[64,40,128]{2,1,0:T(8,128)(2,1)} all-to-all(bf16[64,40,128]{2,1,0:T(8,128)(2,1)S(1)} %second_pass.1), channel_id=1, replica_groups=mesh['y'=4,'x'=4,'far'=8,'pair'=2,'veh'=2] {'y','x','pair','veh'}, dimensions={0} | all-to-all | bytes 1310720 | tf_op jit(solution)/shard_map/all_to_all | solution.py:243
  92.2 1.8 %sum_and_copy.3 = bf16[8,40,128]{2,1,0:T(8,128)(2,1)} custom-call(bf16[64,40,128]{2,1,0:T(8,128)(2,1)} %all_to_all.27.in_ref), custom_call_target="tpu_custom_call" | custom-call | tf_op jit(solution)/shard_map/sum_and_copy/pallas_call | solution.py:111
  94.1 3.4 %all-to-all-start.3 = ((bf16[8,40,128]{2,1,0:T(8,128)(2,1)}), bf16[8,40,128]{2,1,0:T(8,128)(2,1)S(1)}, u32[]{:S(2)}, u32[]{:S(2)}) async-start(bf16[8,40,128]{2,1,0:T(8,128)(2,1)} %sum_and_copy.3), calls=%async_computation.3 | async-start | bytes 163840 | tf_op jit(solution)/shard_map/all_to_all | solution.py:243
  97.4 13.5 %all-to-all-done.3.part_ref = bf16[8,40,128]{2,1,0:T(8,128)(2,1)S(1)} async-done(((bf16[8,40,128]{2,1,0:T(8,128)(2,1)}), bf16[8,40,128]{2,1,0:T(8,128)(2,1)S(1)}, u32[]{:S(2)}, u32[]{:S(2)}) %all-to-all-start.3) | async-done | bytes 81952 | tf_op jit(solution)/shard_map/all_to_all | solution.py:243
  110.9 0.6 copy-done.8
  111.6 2.0 %update_rows.1 = bf16[32,32,128]{2,1,0:T(8,128)(2,1)} custom-call(s32[1]{0:T(128)} %bitcast.where_ref, bf16[8,40,128]{2,1,0:T(8,128)(2,1)} %copy-done.8, bf16[2048,128]{1,0:T(8,128)(2,1)} %veh_ref.3, bf16[128,128]{1,0:T(8,128)(2,1)} %average_ref.1, bf16[128,128]{1,0:T(8,128)(2,1)} %identity_ref.1, f32[1,128]{1,0:T(1,128)} %bitcast.10, ...), custom_call_target="tpu_custom_call" | custom-call | tf_op jit(solution)/shard_map/update_rows/pallas_call | solution.py:222
  113.6 14.2 %all_to_all.28 = bf16[32,32,128]{2,1,0:T(8,128)(2,1)S(1)} all-to-all(bf16[32,32,128]{2,1,0:T(8,128)(2,1)} %update_rows.1), channel_id=1, replica_groups=mesh['y'=4,'x'=4,'far'=8,'pair'=2,'veh'=2] {'y','x','pair'}, dimensions={0} | all-to-all | bytes 524288 | tf_op jit(solution)/shard_map/all_to_all | solution.py:243
  127.7 0.7 copy.10
  (6 shorter events, 0.0 us)
Async XLA Ops:
  0.0 1.2 copy-start.2
  1.2 1.0 copy-start.4
  2.3 0.7 copy-start.5
  14.0 3.2 %copy-start = (bf16[8,2048,256]{2,1,0:T(8,128)(2,1)}, bf16[8,2048,256]{2,1,0:T(8,128)(2,1)S(1)}, u32[]{:S(2)}) copy-start(bf16[8,2048,256]{2,1,0:T(8,128)(2,1)S(1)} %get-tuple-element.8.e_ref) | copy-start | bytes 25165828
  61.3 3.4 %copy-start.1 = (bf16[8,2048,256]{2,1,0:T(8,128)(2,1)S(1)}, bf16[8,2048,256]{2,1,0:T(8,128)(2,1)}, u32[]{:S(2)}) copy-start(bf16[8,2048,256]{2,1,0:T(8,128)(2,1)} %copy-done) | copy-start | bytes 25165828
  64.6 1.2 copy-start.3
  65.9 0.7 copy-start.6
  66.6 0.7 copy-start.7
  94.1 16.9 %all-to-all-start.3 = ((bf16[8,40,128]{2,1,0:T(8,128)(2,1)}), bf16[8,40,128]{2,1,0:T(8,128)(2,1)S(1)}, u32[]{:S(2)}, u32[]{:S(2)}) async-start(bf16[8,40,128]{2,1,0:T(8,128)(2,1)} %sum_and_copy.3), calls=%async_computation.3 | async-start | bytes 163840 | tf_op jit(solution)/shard_map/all_to_all | solution.py:243
  110.9 0.6 copy-start.8

commit v2 on v1

v2 whole, which is shorter than its diff:
```python
import jax
import jax.numpy as jnp
from jax import lax
from jax.experimental import pallas as pl
from jax.experimental.pallas import tpu as pltpu
from jax.sharding import Mesh, PartitionSpec as P

F32 = jnp.float32
BF16 = jnp.bfloat16
LANES = 128
BLOCK = 256
CHUNK = 256
TALL = 512
LOG2E = 1.4426950408889634
ROW_BITS = 90.0
CAP_SCALE = 2.0**-20
WEIGHT_SCALE = 2.0**50
FIRST_LIMIT = 48 << 20
SECOND_LIMIT = 16 << 20
SMALL_LIMIT = 4 << 20
LAST_DIMS = (((1,), (1,)), ((), ()))
VMEM = pl.BlockSpec(memory_space=pltpu.VMEM)
SMEM = pl.BlockSpec(memory_space=pltpu.SMEM)
ANY = pl.BlockSpec(memory_space=pl.ANY)


def diagonal(shape):
    n = len(shape)
    return lax.broadcasted_iota(jnp.int32, shape, n - 2) == lax.broadcasted_iota(
        jnp.int32, shape, n - 1
    )


def on_lanes(column):
    shape = (column.shape[0] // LANES, LANES, LANES)
    return jnp.sum(jnp.where(diagonal(shape), column.reshape(shape), 0.0), axis=1)


def loads_of(ref, b):
    n = BLOCK // LANES
    return jnp.concatenate([ref[pl.ds(b * n + i, 1), :] for i in range(n)], axis=1).astype(F32)


def first_kernel(
    half_ref,
    veh_hbm,
    stop_hbm,
    load_hbm,
    cap_hbm,
    e_ref,
    out_ref,
    turned_ref,
    int_ref,
    veh_ref,
    stop_ref,
    z0_ref,
    z1_ref,
    share_ref,
    sem,
):
    vehicles, width = veh_ref.shape
    scale = LOG2E / width**0.5
    blocks = e_ref.shape[0]
    chunks = vehicles // CHUNK
    own = blocks * BLOCK
    tall = own // LANES
    half = half_ref[0]
    z_refs = (z0_ref, z1_ref)
    mine = pl.ds(pl.multiple_of(half * own, own), own)
    lines = pl.ds(pl.multiple_of(half * tall, tall), tall)
    moves = [
        pltpu.make_async_copy(veh_hbm, veh_ref, sem.at[0]),
        pltpu.make_async_copy(stop_hbm.at[mine], stop_ref, sem.at[1]),
        pltpu.make_async_copy(load_hbm.at[lines], int_ref.at[pl.ds(0, tall)], sem.at[2]),
        pltpu.make_async_copy(cap_hbm, int_ref.at[pl.ds(tall, cap_hbm.shape[0])], sem.at[3]),
    ]
    for move in moves:
        move.start()
    for move in moves:
        move.wait()
    lowest = jnp.full((8, BLOCK), -jnp.inf, F32)

    def turn(b):
        turned = stop_ref[pl.ds(pl.multiple_of(b * BLOCK, BLOCK), BLOCK), :].T
        turned_ref[b] = turned
        return turned

    def scores(z_ref, turned, c, top):
        rows = pl.ds(c * CHUNK, CHUNK)
        z = jnp.dot(veh_ref[rows, :], turned, preferred_element_type=F32)
        z_ref[rows, :] = z
        return jnp.maximum(top, jnp.max(z.reshape(CHUNK // 8, 8, BLOCK), axis=0))

    def exponentials(b, z_ref, top, c, total):
        rows = pl.ds(c * CHUNK, CHUNK)
        e = jnp.exp2((z_ref[rows, :] - top) * scale)
        e_ref[b, rows, :] = e.astype(BF16)
        return total + jnp.sum(e.reshape(CHUNK // 8, 8, BLOCK), axis=0)

    def level(top):
        return jnp.max(top, axis=0, keepdims=True) - ROW_BITS / scale

    def step(b, slot, top, more):
        turned = turn(b + 1) if more else None
        after = lowest
        total = jnp.zeros((8, BLOCK), F32)
        for c in range(chunks):
            if more:
                after = scores(z_refs[1 - slot], turned, c, after)
            total = exponentials(b, z_refs[slot], top, c, total)
        total = jnp.sum(total, axis=0, keepdims=True)
        share = (loads_of(int_ref, b) / total).astype(BF16)
        share_ref[b] = jnp.broadcast_to(share, (LANES, BLOCK))
        return level(after)

    turned = turn(0)
    top = lowest
    for c in range(chunks):
        top = scores(z_refs[0], turned, c, top)
    top = level(top)

    def two(p, top):
        return step(2 * p + 1, 1, step(2 * p, 0, top, True), True)

    top = lax.fori_loop(0, blocks // 2 - 1, two, top)
    top = step(blocks - 2, 0, top, True)
    step(blocks - 1, 1, top, False)

    n = TALL // LANES
    for k in range(vehicles // TALL):
        rows = pl.ds(k * TALL, TALL)
        col = sum(
            lax.dot_general(
                e_ref[b, rows, :], share_ref[b], LAST_DIMS, preferred_element_type=F32
            )
            for b in range(blocks)
        )
        col = on_lanes(col).astype(out_ref.dtype)
        out_ref[:, k * n : (k + 1) * n, :] = jnp.broadcast_to(
            col[None], (out_ref.shape[0], n, LANES)
        )


def first_pass(half, veh, stops, loads, caps, peers):
    vehicles, width = veh.shape
    blocks = stops.shape[0] // 2 // BLOCK
    return pl.pallas_call(
        first_kernel,
        in_specs=[SMEM, ANY, ANY, ANY, ANY],
        out_specs=[VMEM, VMEM, VMEM, VMEM],
        out_shape=[
            pltpu.VMEM((blocks, vehicles, BLOCK), BF16),
            pltpu.VMEM((peers, vehicles // LANES, LANES), BF16),
            pltpu.VMEM((blocks, width, BLOCK), BF16),
            pltpu.VMEM((loads.shape[0] // 2 + caps.shape[0], LANES), jnp.int32),
        ],
        scratch_shapes=[
            pltpu.VMEM((vehicles, width), BF16),
            pltpu.VMEM((blocks * BLOCK, width), BF16),
            pltpu.VMEM((vehicles, BLOCK), F32),
            pltpu.VMEM((vehicles, BLOCK), F32),
            pltpu.VMEM((blocks, LANES, BLOCK), BF16),
            pltpu.SemaphoreType.DMA((4,)),
        ],
        compiler_params=pltpu.CompilerParams(vmem_limit_bytes=FIRST_LIMIT),
        name="first_pass",
    )(half, veh, stops, loads, caps)


def sum_and_copy_kernel(in_ref, out_ref):
    total = jnp.sum(in_ref[...].astype(F32), axis=0)
    out_ref[...] = jnp.broadcast_to(total.astype(out_ref.dtype)[None], out_ref.shape)


def sum_and_copy(parts, copies):
    return pl.pallas_call(
        sum_and_copy_kernel,
        in_specs=[VMEM],
        out_specs=VMEM,
        out_shape=jax.ShapeDtypeStruct((copies,) + parts.shape[1:], parts.dtype),
        compiler_params=pltpu.CompilerParams(vmem_limit_bytes=SMALL_LIMIT),
        name="sum_and_copy",
    )(parts)


def second_kernel(part_ref, turned_ref, int_ref, e_ref, out_ref, g_ref, right_ref):
    blocks, vehicles, _ = e_ref.shape
    width = turned_ref.shape[1]
    lines = vehicles // LANES
    tall = int_ref.shape[0] - lines
    colsum = jnp.sum(part_ref[...].astype(F32), axis=0)
    g = (int_ref[tall:, :].astype(F32) * CAP_SCALE) / colsum
    square = (LANES, LANES)
    eye = diagonal(square)
    for r in range(lines):
        spread = jnp.where(eye, jnp.broadcast_to(g[r : r + 1], square), 0.0)
        column = jnp.sum(spread, axis=1, keepdims=True)
        g_ref[pl.ds(r * LANES, LANES), :] = jnp.broadcast_to(column, square)

    def weigh(b, _):
        total = jnp.zeros((8, BLOCK), F32)
        for c in range(vehicles // CHUNK):
            rows = pl.ds(c * CHUNK, CHUNK)
            g = jnp.concatenate([g_ref[rows, :]] * (BLOCK // LANES), axis=1)
            t = e_ref[b, rows, :].astype(F32) * g
            total = total + jnp.sum(t.reshape(CHUNK // 8, 8, BLOCK), axis=0)
        total = jnp.sum(total, axis=0, keepdims=True)
        weight = (loads_of(int_ref, b) * WEIGHT_SCALE / total).astype(BF16)
        right_ref[b, 0:width, :] = (turned_ref[b].astype(F32) * weight.astype(F32)).astype(BF16)
        right_ref[b, width:, :] = jnp.broadcast_to(weight, (LANES, BLOCK))
        return 0

    lax.fori_loop(0, blocks, weigh, 0)
    peers, own_tall, _ = out_ref.shape
    own = vehicles // peers
    half = peers // 2
    eye = diagonal((own, LANES))
    line = lax.broadcasted_iota(jnp.int32, (own_tall - own, LANES), 0)
    for k in range(vehicles // TALL):
        rows = pl.ds(k * TALL, TALL)
        num = sum(
            lax.dot_general(
                e_ref[b, rows, :], right_ref[b], LAST_DIMS, preferred_element_type=F32
            )
            for b in range(blocks)
        )
        for q in range(TALL // own):
            r = k * (TALL // own) + q
            to = (r % half) * 2 + r // half
            mine = num[q * own : (q + 1) * own]
            out_ref[to, 0:own, :] = mine[:, 0:width].astype(BF16)
            den = jnp.sum(jnp.where(eye, mine[:, width:], 0.0), axis=0, keepdims=True)
            high = den.astype(BF16).astype(F32)
            tail = jnp.where(line == 0, high, jnp.where(line == 1, den - high, 0.0))
            out_ref[to, own:own_tall, :] = tail.astype(BF16)


def second_pass(parts, turned, ints, e, peers):
    blocks, vehicles, _ = e.shape
    width = turned.shape[1]
    return pl.pallas_call(
        second_kernel,
        in_specs=[VMEM, VMEM, VMEM, VMEM],
        out_specs=VMEM,
        out_shape=jax.ShapeDtypeStruct((peers, vehicles // peers + 8, width), BF16),
        scratch_shapes=[
            pltpu.VMEM((vehicles, LANES), F32),
            pltpu.VMEM((blocks, width + LANES, BLOCK), BF16),
        ],
        compiler_params=pltpu.CompilerParams(vmem_limit_bytes=SECOND_LIMIT),
        name="second_pass",
    )(parts, turned, ints, e)


def update_kernel(
    where_ref, part_ref, veh_ref, average_ref, identity_ref, offset_ref, projector_ref, out_ref
):
    own = part_ref.shape[1] - 8
    total = jnp.sum(part_ref[...].astype(F32), axis=0)
    den = total[own : own + 1, :] + total[own + 1 : own + 2, :]
    shape = (own, LANES)
    spread = jnp.where(diagonal(shape), jnp.broadcast_to(den, shape), 0.0)
    den = jnp.sum(spread, axis=1, keepdims=True)
    centroid = (total[0:own] / den).astype(BF16)
    rows = veh_ref[pl.ds(pl.multiple_of(where_ref[0] * own, own), own), :]
    pre = jnp.dot(centroid, average_ref[...], preferred_element_type=F32)
    pre = pre + jnp.dot(rows, identity_ref[...], preferred_element_type=F32) + offset_ref[...]
    hidden = jax.nn.silu(pre).astype(BF16)
    update = jnp.dot(hidden, projector_ref[...], preferred_element_type=F32)
    new = (rows.astype(F32) + update).astype(BF16)
    for r in range(out_ref.shape[0] // own):
        out_ref[pl.ds(r * own, own), :] = new


def update_rows(where, parts, veh, average, identity, offset, projector, copies):
    own = parts.shape[1] - 8
    return pl.pallas_call(
        update_kernel,
        in_specs=[SMEM] + [VMEM] * 6,
        out_specs=VMEM,
        out_shape=jax.ShapeDtypeStruct((copies * own, veh.shape[1]), BF16),
        compiler_params=pltpu.CompilerParams(vmem_limit_bytes=SMALL_LIMIT),
        name="update_rows",
    )(where, parts, veh, average, identity, offset, projector)


def swap(array, axes):
    return lax.all_to_all(array, axes, 0, 0, tiled=True)


def solution(mesh):
    stops_n = mesh.shape["stops"]
    y = x = 4
    pair = 2
    far = stops_n // (y * x * pair)
    inner = Mesh(
        mesh.devices.reshape(y, x, far, pair, mesh.shape["veh"]), ("y", "x", "far", "pair", "veh")
    )

    def on_device(
        customer_features,
        customer_loads,
        truck_limits,
        truck_features,
        customer_average_matrix,
        truck_identity_matrix,
        hidden_offset,
        output_projector,
    ):
        core = lax.axis_index("veh")
        half = core.astype(jnp.int32).reshape(1)
        near = (lax.axis_index("y") * x + lax.axis_index("x")) * pair + lax.axis_index("pair")
        chips = y * x * pair
        where = (core * chips + near).astype(jnp.int32).reshape(1)
        loads = customer_loads.reshape(-1, LANES)
        caps = truck_limits.reshape(-1, LANES)

        e, col, turned, ints = first_pass(
            half, truck_features, customer_features, loads, caps, y * x * 2
        )
        col = swap(col, ("y", "x", "veh"))
        col = swap(sum_and_copy(col, far * pair), ("far", "pair"))
        parts = second_pass(col, turned, ints, e, chips * 2)
        parts = swap(parts, ("y", "x", "pair", "veh"))
        parts = swap(sum_and_copy(parts, far), "far")
        new = update_rows(
            where,
            parts,
            truck_features,
            customer_average_matrix,
            truck_identity_matrix,
            hidden_offset.reshape(1, -1),
            output_projector,
            chips,
        )
        return swap(new, ("y", "x", "pair"))

    split = ("y", "x", "far", "pair")
    placed = (P(split, None), P(split), P(), P(), P(), P(), P(), P())
    return jax.shard_map(
        on_device, mesh=inner, in_specs=placed, out_specs=P("veh", None), check_vma=False
    )
```

time: 129 us -> 107 us (0.83)
  local copies, waits for them, and re-layouts: 13.5 us -> 0.72 us
  Pallas kernels: 22.8 us -> 14.7 us
    unnamed x19 -> x11, local copies, waits for them, and re-layouts: 13.5 us -> 0.72 us
    pallas_call x5, Pallas kernels: 22.8 us -> 14.7 us  [the longest x1 8.94 us: first_pass(): pl.pallas_call(first_kernel, in_specs=[SMEM, ANY, ANY, ANY, ANY], out_spe...]
where the time goes in v2:
time: 107 us
  blocking collectives  74.5 us (70%)
  Pallas kernels  14.7 us (14%)
  waiting for transfers between devices  13.5 us (13%)
  starting transfers between devices  3.36 us (3%)
    all_to_all x4, blocking collectives, swap(): return lax.all_to_all(array, axes, 0, 0, tiled=True)  74.5 us
    all_to_all x1, waiting for transfers between devices, swap(): return lax.all_to_all(array, axes, 0, 0, tiled=True)  13.5 us
    pallas_call x1, Pallas kernels, first_pass(): pl.pallas_call(first_kernel, in_specs=[SMEM, ANY, ANY, ANY, ANY], out_spe...  8.94 us
    pallas_call x1, Pallas kernels, second_pass(): pl.pallas_call(second_kernel, in_specs=[VMEM, VMEM, VMEM, VMEM], out_spec...  4.62 us
    all_to_all x1, starting transfers between devices, swap(): return lax.all_to_all(array, axes, 0, 0, tiled=True)  3.36 us
  transfers between devices with their start and end apart: 1, of which 1 were waited for; matrix products, arithmetic and copies ran while one was open for 0% of the time, Pallas kernels for 0%

profile of v2, /device:TPU:2, one launch (start us, length us, event | category | flops | bytes accessed | tf_op | source)
XLA Modules:
  0.0 106.9 jit_solution(18361823933779640281)
XLA Ops:
  0.0 0.0 copy-start
  0.0 0.0 copy-start.3
  0.0 0.0 copy-start.4
  0.0 0.0 copy-start.2
  0.0 0.0 copy-start.1
  0.0 8.9 %first_pass.1 = (bf16[8,2048,256]{2,1,0:T(8,128)(2,1)S(1)}, bf16[32,16,128]{2,1,0:T(8,128)(2,1)S(1)}, bf16[8,128,256]{2,1,0:T(8,128)(2,1)S(1)}, s32[32,128]{1,0:T(8,128)S(1)}) custom-call(s32[1]{0:T(128)} %bitcast.1.half_ref, bf16[2048,128]{1,0:T(8,128)(2,1)} %veh_ref.1, bf16[4096,128]{1,0:T(8,128)(2,1)} %stop_hbm.1, s32[32,128]{1,0:T(8,128)} %bitcast.10, ...), custom_call_target="tpu_custom_call" | custom-call | tf_op jit(solution)/shard_map/first_pass/pallas_call | solution.py:147
  9.0 15.3 %all_to_all.32.in_ref = bf16[32,16,128]{2,1,0:T(8,128)(2,1)S(1)} all-to-all(bf16[32,16,128]{2,1,0:T(8,128)(2,1)S(1)} %get-tuple-element.9), channel_id=1, replica_groups=mesh['y'=4,'x'=4,'far'=8,'pair'=2,'veh'=2] {'y','x','veh'}, dimensions={0} | all-to-all | bytes 262144 | tf_op jit(solution)/shard_map/all_to_all | solution.py:288
  24.3 26.9 %all_to_all.33.part_ref = bf16[16,16,128]{2,1,0:T(8,128)(2,1)S(1)} all-to-all(bf16[16,16,128]{2,1,0:T(8,128)(2,1)S(1)} %sum_and_copy.2), channel_id=1, replica_groups=mesh['y'=4,'x'=4,'far'=8,'pair'=2,'veh'=2] {'far','pair'}, dimensions={0} | all-to-all | bytes 131072 | tf_op jit(solution)/shard_map/all_to_all | solution.py:288
  51.1 4.6 %second_pass.1 = bf16[64,40,128]{2,1,0:T(8,128)(2,1)S(1)} custom-call(bf16[16,16,128]{2,1,0:T(8,128)(2,1)S(1)} %all_to_all.33.part_ref, bf16[8,128,256]{2,1,0:T(8,128)(2,1)S(1)} %get-tuple-element.10.turned_ref, s32[32,128]{1,0:T(8,128)S(1)} %get-tuple-element.11.int_ref, bf16[8,2048,256]{2,1,0:T(8,128)(2,1)S(1)} %get-tuple-element.12.e_ref), custom_call_target="tpu_custom_call" | custom-call | tf_op jit(solution)/shard_map/second_pass/pallas_call | solution.py:241
  55.8 18.4 %all_to_all.34.in_ref = bf16[64,40,128]{2,1,0:T(8,128)(2,1)S(1)} all-to-all(bf16[64,40,128]{2,1,0:T(8,128)(2,1)S(1)} %second_pass.1), channel_id=1, replica_groups=mesh['y'=4,'x'=4,'far'=8,'pair'=2,'veh'=2] {'y','x','pair','veh'}, dimensions={0} | all-to-all | bytes 1310720 | tf_op jit(solution)/shard_map/all_to_all | solution.py:288
  74.2 0.8 sum_and_copy.3
  75.0 3.4 %all-to-all-start.3 = ((bf16[8,40,128]{2,1,0:T(8,128)(2,1)}), bf16[8,40,128]{2,1,0:T(8,128)(2,1)S(1)}, u32[]{:S(2)}, u32[]{:S(2)}) async-start(bf16[8,40,128]{2,1,0:T(8,128)(2,1)} %sum_and_copy.3), calls=%async_computation.3 | async-start | bytes 163840 | tf_op jit(solution)/shard_map/all_to_all | solution.py:288
  78.3 13.5 %all-to-all-done.3.part_ref = bf16[8,40,128]{2,1,0:T(8,128)(2,1)S(1)} async-done(((bf16[8,40,128]{2,1,0:T(8,128)(2,1)}), bf16[8,40,128]{2,1,0:T(8,128)(2,1)S(1)}, u32[]{:S(2)}, u32[]{:S(2)}) %all-to-all-start.3) | async-done | bytes 81952 | tf_op jit(solution)/shard_map/all_to_all | solution.py:288
  91.8 0.0 copy-done
  91.8 0.0 copy-done.3
  91.8 0.0 copy-done.4
  91.8 0.0 copy-done.2
  91.9 0.0 copy-done.1
  91.9 0.4 update_rows.1
  92.2 14.0 %all_to_all.35 = bf16[32,32,128]{2,1,0:T(8,128)(2,1)S(1)} all-to-all(bf16[32,32,128]{2,1,0:T(8,128)(2,1)S(1)} %bitcast.7), channel_id=1, replica_groups=mesh['y'=4,'x'=4,'far'=8,'pair'=2,'veh'=2] {'y','x','pair'}, dimensions={0} | all-to-all | bytes 524288 | tf_op jit(solution)/shard_map/all_to_all | solution.py:288
  106.2 0.7 copy.10
  (1 shorter events, 0.0 us)
Async XLA Ops:
  0.0 91.8 %copy-start = (bf16[2048,128]{1,0:T(8,128)(2,1)S(1)}, bf16[2048,128]{1,0:T(8,128)(2,1)}, u32[]{:S(2)}) copy-start(bf16[2048,128]{1,0:T(8,128)(2,1)} %veh_ref.1) | copy-start | bytes 1572868
  0.0 91.8 %copy-start.3 = (bf16[128,128]{1,0:T(8,128)(2,1)S(1)}, bf16[128,128]{1,0:T(8,128)(2,1)}, u32[]{:S(2)}) copy-start(bf16[128,128]{1,0:T(8,128)(2,1)} %projector_ref.1) | copy-start | bytes 98308
  0.0 91.8 %copy-start.4 = (f32[128]{0:T(128)S(1)}, f32[128]{0:T(128)}, u32[]{:S(2)}) copy-start(f32[128]{0:T(128)} %param.14) | copy-start | bytes 1540
  0.0 91.8 %copy-start.2 = (bf16[128,128]{1,0:T(8,128)(2,1)S(1)}, bf16[128,128]{1,0:T(8,128)(2,1)}, u32[]{:S(2)}) copy-start(bf16[128,128]{1,0:T(8,128)(2,1)} %identity_ref.1) | copy-start | bytes 98308
  0.0 91.8 %copy-start.1 = (bf16[128,128]{1,0:T(8,128)(2,1)S(1)}, bf16[128,128]{1,0:T(8,128)(2,1)}, u32[]{:S(2)}) copy-start(bf16[128,128]{1,0:T(8,128)(2,1)} %average_ref.1) | copy-start | bytes 98308
  75.0 16.9 %all-to-all-start.3 = ((bf16[8,40,128]{2,1,0:T(8,128)(2,1)}), bf16[8,40,128]{2,1,0:T(8,128)(2,1)S(1)}, u32[]{:S(2)}, u32[]{:S(2)}) async-start(bf16[8,40,128]{2,1,0:T(8,128)(2,1)} %sum_and_copy.3), calls=%async_computation.3 | async-start | bytes 163840 | tf_op jit(solution)/shard_map/all_to_all | solution.py:288

commit v3 on v2

--- a/solution.py
+++ b/solution.py
@@ -1,3 +1,5 @@
+import functools
+
 import jax
 import jax.numpy as jnp
 from jax import lax
@@ -29,11 +31,6 @@
     return lax.broadcasted_iota(jnp.int32, shape, n - 2) == lax.broadcasted_iota(
         jnp.int32, shape, n - 1
     )
-
-
-def on_lanes(column):
-    shape = (column.shape[0] // LANES, LANES, LANES)
-    return jnp.sum(jnp.where(diagonal(shape), column.reshape(shape), 0.0), axis=1)
 
 
 def loads_of(ref, b):
@@ -126,19 +123,15 @@
     top = step(blocks - 2, 0, top, True)
     step(blocks - 1, 1, top, False)
 
-    n = TALL // LANES
-    for k in range(vehicles // TALL):
-        rows = pl.ds(k * TALL, TALL)
-        col = sum(
-            lax.dot_general(
-                e_ref[b, rows, :], share_ref[b], LAST_DIMS, preferred_element_type=F32
-            )
-            for b in range(blocks)
-        )
-        col = on_lanes(col).astype(out_ref.dtype)
-        out_ref[:, k * n : (k + 1) * n, :] = jnp.broadcast_to(
-            col[None], (out_ref.shape[0], n, LANES)
-        )
+    for k in range(vehicles // LANES):
+        rows = pl.ds(k * LANES, LANES)
+        col = jnp.zeros((LANES, LANES), F32)
+        for b in range(blocks):
+            t = e_ref[b, rows, :] * share_ref[b]
+            t = t[:, 0:LANES] + t[:, LANES:BLOCK]
+            col = col + t.astype(F32)
+        col = jnp.sum(col.T, axis=0, keepdims=True).astype(out_ref.dtype)
+        out_ref[:, k : k + 1, :] = jnp.broadcast_to(col[None], (out_ref.shape[0], 1, LANES))
 
 
 def first_pass(half, veh, stops, loads, caps, peers):
@@ -195,22 +188,20 @@
     for r in range(lines):
         spread = jnp.where(eye, jnp.broadcast_to(g[r : r + 1], square), 0.0)
         column = jnp.sum(spread, axis=1, keepdims=True)
-        g_ref[pl.ds(r * LANES, LANES), :] = jnp.broadcast_to(column, square)
-
-    def weigh(b, _):
-        total = jnp.zeros((8, BLOCK), F32)
+        g_ref[pl.ds(r * LANES, LANES), :] = jnp.broadcast_to(column, square).astype(BF16)
+
+    for b in range(blocks):
+        total = jnp.zeros((16, BLOCK), F32)
         for c in range(vehicles // CHUNK):
             rows = pl.ds(c * CHUNK, CHUNK)
             g = jnp.concatenate([g_ref[rows, :]] * (BLOCK // LANES), axis=1)
-            t = e_ref[b, rows, :].astype(F32) * g
-            total = total + jnp.sum(t.reshape(CHUNK // 8, 8, BLOCK), axis=0)
+            t = (e_ref[b, rows, :] * g).reshape(CHUNK // 32, 2, 16, BLOCK)
+            t = (t[:, 0] + t[:, 1]).astype(F32)
+            total = total + jnp.sum(t, axis=0)
         total = jnp.sum(total, axis=0, keepdims=True)
         weight = (loads_of(int_ref, b) * WEIGHT_SCALE / total).astype(BF16)
         right_ref[b, 0:width, :] = (turned_ref[b].astype(F32) * weight.astype(F32)).astype(BF16)
         right_ref[b, width:, :] = jnp.broadcast_to(weight, (LANES, BLOCK))
-        return 0
-
-    lax.fori_loop(0, blocks, weigh, 0)
     peers, own_tall, _ = out_ref.shape
     own = vehicles // peers
     half = peers // 2
@@ -244,7 +235,7 @@
         out_specs=VMEM,
         out_shape=jax.ShapeDtypeStruct((peers, vehicles // peers + 8, width), BF16),
         scratch_shapes=[
-            pltpu.VMEM((vehicles, LANES), F32),
+            pltpu.VMEM((vehicles, LANES), BF16),
             pltpu.VMEM((blocks, width + LANES, BLOCK), BF16),
         ],
         compiler_params=pltpu.CompilerParams(vmem_limit_bytes=SECOND_LIMIT),
@@ -253,7 +244,7 @@
 
 
 def update_kernel(
-    where_ref, part_ref, veh_ref, average_ref, identity_ref, offset_ref, projector_ref, out_ref
+    chips, part_ref, veh_ref, average_ref, identity_ref, offset_ref, projector_ref, out_ref
 ):
     own = part_ref.shape[1] - 8
     total = jnp.sum(part_ref[...].astype(F32), axis=0)
@@ -262,7 +253,10 @@
     spread = jnp.where(diagonal(shape), jnp.broadcast_to(den, shape), 0.0)
     den = jnp.sum(spread, axis=1, keepdims=True)
     centroid = (total[0:own] / den).astype(BF16)
-    rows = veh_ref[pl.ds(pl.multiple_of(where_ref[0] * own, own), own), :]
+    y, x, pair, core = (lax.axis_index(name) for name in ("y", "x", "pair", "veh"))
+    x_n, pair_n = lax.axis_size("x"), lax.axis_size("pair")
+    where = core * chips + (y * x_n + x) * pair_n + pair
+    rows = veh_ref[pl.ds(pl.multiple_of(where * own, own), own), :]
     pre = jnp.dot(centroid, average_ref[...], preferred_element_type=F32)
     pre = pre + jnp.dot(rows, identity_ref[...], preferred_element_type=F32) + offset_ref[...]
     hidden = jax.nn.silu(pre).astype(BF16)
@@ -272,16 +266,16 @@
         out_ref[pl.ds(r * own, own), :] = new
 
 
-def update_rows(where, parts, veh, average, identity, offset, projector, copies):
+def update_rows(parts, veh, average, identity, offset, projector, copies):
     own = parts.shape[1] - 8
     return pl.pallas_call(
-        update_kernel,
-        in_specs=[SMEM] + [VMEM] * 6,
+        functools.partial(update_kernel, copies),
+        in_specs=[VMEM] * 6,
         out_specs=VMEM,
         out_shape=jax.ShapeDtypeStruct((copies * own, veh.shape[1]), BF16),
         compiler_params=pltpu.CompilerParams(vmem_limit_bytes=SMALL_LIMIT),
         name="update_rows",
-    )(where, parts, veh, average, identity, offset, projector)
+    )(parts, veh, average, identity, offset, projector)
 
 
 def swap(array, axes):
@@ -309,22 +303,19 @@
     ):
         core = lax.axis_index("veh")
         half = core.astype(jnp.int32).reshape(1)
-        near = (lax.axis_index("y") * x + lax.axis_index("x")) * pair + lax.axis_index("pair")
         chips = y * x * pair
-        where = (core * chips + near).astype(jnp.int32).reshape(1)
         loads = customer_loads.reshape(-1, LANES)
         caps = truck_limits.reshape(-1, LANES)
 
         e, col, turned, ints = first_pass(
-            half, truck_features, customer_features, loads, caps, y * x * 2
+            half, truck_features, customer_features, loads, caps, far * pair
         )
-        col = swap(col, ("y", "x", "veh"))
-        col = swap(sum_and_copy(col, far * pair), ("far", "pair"))
+        col = swap(col, ("far", "pair"))
+        col = swap(sum_and_copy(col, y * x * 2), ("y", "x", "veh"))
         parts = second_pass(col, turned, ints, e, chips * 2)
         parts = swap(parts, ("y", "x", "pair", "veh"))
         parts = swap(sum_and_copy(parts, far), "far")
         new = update_rows(
-            where,
             parts,
             truck_features,
             customer_average_matrix,

time: 107 us -> 105 us (0.981)
  blocking collectives: 74.5 us -> 90.8 us
  waiting for transfers between devices: 13.5 us -> 0 us
  starting transfers between devices: 3.36 us -> 0 us
  Pallas kernels: 14.7 us -> 12.8 us
    all_to_all x4 -> x5, blocking collectives: 74.5 us -> 90.8 us  [swap(): return lax.all_to_all(array, axes, 0, 0, tiled=True)]
    all_to_all x1 -> x0, waiting for transfers between devices: 13.5 us -> none  [swap(): return lax.all_to_all(array, axes, 0, 0, tiled=True)]
    all_to_all x1 -> x0, starting transfers between devices: 3.36 us -> none  [swap(): return lax.all_to_all(array, axes, 0, 0, tiled=True)]
  transfers between devices with their start and end apart: 1 -> 0, of which waited for: 1 -> 0; matrix products, arithmetic and copies ran while one was open for 0% -> 0% of each run, Pallas kernels for 0% -> 0%
where the time goes in v3:
time: 105 us; the launch traced here: 104 us
  blocking collectives  90.8 us (86%)
  Pallas kernels  12.8 us (12%)
    all_to_all x5, blocking collectives, swap(): return lax.all_to_all(array, axes, 0, 0, tiled=True)  90.8 us
    pallas_call x1, Pallas kernels, first_pass(): pl.pallas_call(first_kernel, in_specs=[SMEM, ANY, ANY, ANY, ANY], out_spe...  8.51 us
    pallas_call x1, Pallas kernels, second_pass(): pl.pallas_call(second_kernel, in_specs=[VMEM, VMEM, VMEM, VMEM], out_spec...  3.76 us

profile of v3, /device:TPU:2, one launch (start us, length us, event | category | flops | bytes accessed | tf_op | source)
XLA Modules:
  0.0 104.4 jit_solution(11899995502589166370)
XLA Ops:
  0.0 0.0 copy-start
  0.0 0.0 copy-start.3
  0.0 0.0 copy-start.4
  0.0 0.0 copy-start.2
  0.0 0.0 copy-start.1
  0.0 8.5 %first_pass.1 = (bf16[8,2048,256]{2,1,0:T(8,128)(2,1)S(1)}, bf16[16,16,128]{2,1,0:T(8,128)(2,1)S(1)}, bf16[8,128,256]{2,1,0:T(8,128)(2,1)S(1)}, s32[32,128]{1,0:T(8,128)S(1)}) custom-call(s32[1]{0:T(128)} %bitcast.half_ref, bf16[2048,128]{1,0:T(8,128)(2,1)} %veh_ref.1, bf16[4096,128]{1,0:T(8,128)(2,1)} %stop_hbm.1, s32[32,128]{1,0:T(8,128)} %bitcast.9, ...), custom_call_target="tpu_custom_call" | custom-call | tf_op jit(solution)/shard_map/first_pass/pallas_call | solution.py:140
  8.6 27.7 %all_to_all.32.in_ref = bf16[16,16,128]{2,1,0:T(8,128)(2,1)S(1)} all-to-all(bf16[16,16,128]{2,1,0:T(8,128)(2,1)S(1)} %get-tuple-element.9), channel_id=1, replica_groups=mesh['y'=4,'x'=4,'far'=8,'pair'=2,'veh'=2] {'far','pair'}, dimensions={0} | all-to-all | bytes 131072 | tf_op jit(solution)/shard_map/all_to_all | solution.py:282
  36.3 14.0 %all_to_all.33.part_ref = bf16[32,16,128]{2,1,0:T(8,128)(2,1)S(1)} all-to-all(bf16[32,16,128]{2,1,0:T(8,128)(2,1)S(1)} %sum_and_copy.2), channel_id=1, replica_groups=mesh['y'=4,'x'=4,'far'=8,'pair'=2,'veh'=2] {'y','x','veh'}, dimensions={0} | all-to-all | bytes 262144 | tf_op jit(solution)/shard_map/all_to_all | solution.py:282
  50.3 3.8 %second_pass.1 = bf16[64,40,128]{2,1,0:T(8,128)(2,1)S(1)} custom-call(bf16[32,16,128]{2,1,0:T(8,128)(2,1)S(1)} %all_to_all.33.part_ref, bf16[8,128,256]{2,1,0:T(8,128)(2,1)S(1)} %get-tuple-element.10.turned_ref, s32[32,128]{1,0:T(8,128)S(1)} %get-tuple-element.11.int_ref, bf16[8,2048,256]{2,1,0:T(8,128)(2,1)S(1)} %get-tuple-element.12.e_ref), custom_call_target="tpu_custom_call" | custom-call | tf_op jit(solution)/shard_map/second_pass/pallas_call | solution.py:232
  54.1 18.4 %all_to_all.34.in_ref = bf16[64,40,128]{2,1,0:T(8,128)(2,1)S(1)} all-to-all(bf16[64,40,128]{2,1,0:T(8,128)(2,1)S(1)} %second_pass.1), channel_id=1, replica_groups=mesh['y'=4,'x'=4,'far'=8,'pair'=2,'veh'=2] {'y','x','pair','veh'}, dimensions={0} | all-to-all | bytes 1310720 | tf_op jit(solution)/shard_map/all_to_all | solution.py:282
  72.5 0.1 sum_and_copy.3
  72.6 17.0 %all_to_all.35.part_ref = bf16[8,40,128]{2,1,0:T(8,128)(2,1)S(1)} all-to-all(bf16[8,40,128]{2,1,0:T(8,128)(2,1)S(1)} %sum_and_copy.3), channel_id=1, replica_groups=mesh['y'=4,'x'=4,'far'=8,'pair'=2,'veh'=2] {'far'}, dimensions={0} | all-to-all | bytes 163840 | tf_op jit(solution)/shard_map/all_to_all | solution.py:282
  89.6 0.0 copy-done
  89.6 0.0 copy-done.3
  89.6 0.0 copy-done.4
  89.6 0.0 copy-done.2
  89.6 0.0 copy-done.1
  89.6 0.4 update_rows.1
  90.0 13.7 %all_to_all.36 = bf16[32,32,128]{2,1,0:T(8,128)(2,1)S(1)} all-to-all(bf16[32,32,128]{2,1,0:T(8,128)(2,1)S(1)} %bitcast.6), channel_id=1, replica_groups=mesh['y'=4,'x'=4,'far'=8,'pair'=2,'veh'=2] {'y','x','pair'}, dimensions={0} | all-to-all | bytes 524288 | tf_op jit(solution)/shard_map/all_to_all | solution.py:282
  103.7 0.7 copy.10
  (1 shorter events, 0.0 us)
Async XLA Ops:
  0.0 89.6 %copy-start = (bf16[2048,128]{1,0:T(8,128)(2,1)S(1)}, bf16[2048,128]{1,0:T(8,128)(2,1)}, u32[]{:S(2)}) copy-start(bf16[2048,128]{1,0:T(8,128)(2,1)} %veh_ref.1) | copy-start | bytes 1572868
  0.0 89.6 %copy-start.3 = (bf16[128,128]{1,0:T(8,128)(2,1)S(1)}, bf16[128,128]{1,0:T(8,128)(2,1)}, u32[]{:S(2)}) copy-start(bf16[128,128]{1,0:T(8,128)(2,1)} %projector_ref.1) | copy-start | bytes 98308
  0.0 89.6 %copy-start.4 = (f32[128]{0:T(128)S(1)}, f32[128]{0:T(128)}, u32[]{:S(2)}) copy-start(f32[128]{0:T(128)} %param.14) | copy-start | bytes 1540
  0.0 89.6 %copy-start.2 = (bf16[128,128]{1,0:T(8,128)(2,1)S(1)}, bf16[128,128]{1,0:T(8,128)(2,1)}, u32[]{:S(2)}) copy-start(bf16[128,128]{1,0:T(8,128)(2,1)} %identity_ref.1) | copy-start | bytes 98308
  0.0 89.6 %copy-start.1 = (bf16[128,128]{1,0:T(8,128)(2,1)S(1)}, bf16[128,128]{1,0:T(8,128)(2,1)}, u32[]{:S(2)}) copy-start(bf16[128,128]{1,0:T(8,128)(2,1)} %average_ref.1) | copy-start | bytes 98308

commit v4 on v3

--- a/solution.py
+++ b/solution.py
@@ -71,31 +71,33 @@
         pltpu.make_async_copy(load_hbm.at[lines], int_ref.at[pl.ds(0, tall)], sem.at[2]),
         pltpu.make_async_copy(cap_hbm, int_ref.at[pl.ds(tall, cap_hbm.shape[0])], sem.at[3]),
     ]
-    for move in moves:
-        move.start()
-    for move in moves:
+    for i in (1, 0, 2, 3):
+        moves[i].start()
+    moves[1].wait()
+    for b in range(blocks):
+        turned_ref[b] = stop_ref[pl.ds(b * BLOCK, BLOCK), :].T
+    for move in (moves[0], *moves[2:]):
         move.wait()
     lowest = jnp.full((8, BLOCK), -jnp.inf, F32)
 
     def turn(b):
-        turned = stop_ref[pl.ds(pl.multiple_of(b * BLOCK, BLOCK), BLOCK), :].T
-        turned_ref[b] = turned
-        return turned
+        return turned_ref[b]
 
     def scores(z_ref, turned, c, top):
         rows = pl.ds(c * CHUNK, CHUNK)
         z = jnp.dot(veh_ref[rows, :], turned, preferred_element_type=F32)
+        z = z * scale
         z_ref[rows, :] = z
         return jnp.maximum(top, jnp.max(z.reshape(CHUNK // 8, 8, BLOCK), axis=0))
 
     def exponentials(b, z_ref, top, c, total):
         rows = pl.ds(c * CHUNK, CHUNK)
-        e = jnp.exp2((z_ref[rows, :] - top) * scale)
+        e = jnp.exp2(z_ref[rows, :] - top)
         e_ref[b, rows, :] = e.astype(BF16)
         return total + jnp.sum(e.reshape(CHUNK // 8, 8, BLOCK), axis=0)
 
     def level(top):
-        return jnp.max(top, axis=0, keepdims=True) - ROW_BITS / scale
+        return jnp.max(top, axis=0, keepdims=True) - ROW_BITS
 
     def step(b, slot, top, more):
         turned = turn(b + 1) if more else None
@@ -176,7 +178,7 @@
     )(parts)
 
 
-def second_kernel(part_ref, turned_ref, int_ref, e_ref, out_ref, g_ref, right_ref):
+def second_kernel(part_ref, turned_ref, int_ref, e_ref, own_ref, other_ref, g_ref, right_ref):
     blocks, vehicles, _ = e_ref.shape
     width = turned_ref.shape[1]
     lines = vehicles // LANES
@@ -202,28 +204,29 @@
         weight = (loads_of(int_ref, b) * WEIGHT_SCALE / total).astype(BF16)
         right_ref[b, 0:width, :] = (turned_ref[b].astype(F32) * weight.astype(F32)).astype(BF16)
         right_ref[b, width:, :] = jnp.broadcast_to(weight, (LANES, BLOCK))
-    peers, own_tall, _ = out_ref.shape
-    own = vehicles // peers
-    half = peers // 2
+    peers, own_tall, _ = own_ref.shape
+    half = vehicles // 2
+    own = half // peers
     eye = diagonal((own, LANES))
     line = lax.broadcasted_iota(jnp.int32, (own_tall - own, LANES), 0)
-    for k in range(vehicles // TALL):
-        rows = pl.ds(k * TALL, TALL)
-        num = sum(
-            lax.dot_general(
-                e_ref[b, rows, :], right_ref[b], LAST_DIMS, preferred_element_type=F32
+    core = lax.axis_index("veh")
+    for out_ref, first in ((other_ref, (1 - core) * half), (own_ref, core * half)):
+        for k in range(half // TALL):
+            rows = pl.ds(pl.multiple_of(first + k * TALL, TALL), TALL)
+            num = sum(
+                lax.dot_general(
+                    e_ref[b, rows, :], right_ref[b], LAST_DIMS, preferred_element_type=F32
+                )
+                for b in range(blocks)
             )
-            for b in range(blocks)
-        )
-        for q in range(TALL // own):
-            r = k * (TALL // own) + q
-            to = (r % half) * 2 + r // half
-            mine = num[q * own : (q + 1) * own]
-            out_ref[to, 0:own, :] = mine[:, 0:width].astype(BF16)
-            den = jnp.sum(jnp.where(eye, mine[:, width:], 0.0), axis=0, keepdims=True)
-            high = den.astype(BF16).astype(F32)
-            tail = jnp.where(line == 0, high, jnp.where(line == 1, den - high, 0.0))
-            out_ref[to, own:own_tall, :] = tail.astype(BF16)
+            for q in range(TALL // own):
+                to = k * (TALL // own) + q
+                mine = num[q * own : (q + 1) * own]
+                out_ref[to, 0:own, :] = mine[:, 0:width].astype(out_ref.dtype)
+                den = jnp.sum(jnp.where(eye, mine[:, width:], 0.0), axis=0, keepdims=True)
+                high = den.astype(BF16).astype(F32)
+                tail = jnp.where(line == 0, high, jnp.where(line == 1, den - high, 0.0))
+                out_ref[to, own:own_tall, :] = tail.astype(out_ref.dtype)
 
 
 def second_pass(parts, turned, ints, e, peers):
@@ -232,8 +235,11 @@
     return pl.pallas_call(
         second_kernel,
         in_specs=[VMEM, VMEM, VMEM, VMEM],
-        out_specs=VMEM,
-        out_shape=jax.ShapeDtypeStruct((peers, vehicles // peers + 8, width), BF16),
+        out_specs=[VMEM, VMEM],
+        out_shape=[
+            jax.ShapeDtypeStruct((peers, vehicles // (2 * peers) + 8, width), F32),
+            jax.ShapeDtypeStruct((peers, vehicles // (2 * peers) + 8, width), BF16),
+        ],
         scratch_shapes=[
             pltpu.VMEM((vehicles, LANES), BF16),
             pltpu.VMEM((blocks, width + LANES, BLOCK), BF16),
@@ -241,6 +247,29 @@
         compiler_params=pltpu.CompilerParams(vmem_limit_bytes=SECOND_LIMIT),
         name="second_pass",
     )(parts, turned, ints, e)
+
+
+def join_kernel(own_ref, sent_ref, out_ref):
+    own = own_ref[...]
+    tall = own.shape[1]
+    total = own + sent_ref[1 - lax.axis_index("veh")].astype(F32)
+    den = total[:, tall - 8 : tall - 7] + total[:, tall - 7 : tall - 6]
+    high = den.astype(BF16).astype(F32)
+    line = lax.broadcasted_iota(jnp.int32, (1, 8, LANES), 1)
+    tail = jnp.where(line == 0, high, jnp.where(line == 1, den - high, 0.0))
+    out_ref[:, : tall - 8, :] = total[:, : tall - 8].astype(BF16)
+    out_ref[:, tall - 8 :, :] = tail.astype(BF16)
+
+
+def join_cores(own, sent):
+    return pl.pallas_call(
+        join_kernel,
+        in_specs=[VMEM, VMEM],
+        out_specs=VMEM,
+        out_shape=jax.ShapeDtypeStruct(own.shape, BF16),
+        compiler_params=pltpu.CompilerParams(vmem_limit_bytes=SMALL_LIMIT),
+        name="join_cores",
+    )(own, sent)
 
 
 def update_kernel(
@@ -312,8 +341,9 @@
         )
         col = swap(col, ("far", "pair"))
         col = swap(sum_and_copy(col, y * x * 2), ("y", "x", "veh"))
-        parts = second_pass(col, turned, ints, e, chips * 2)
-        parts = swap(parts, ("y", "x", "pair", "veh"))
+        own, other = second_pass(col, turned, ints, e, chips)
+        parts = join_cores(own, lax.all_gather(other, "veh"))
+        parts = swap(parts, ("y", "x", "pair"))
         parts = swap(sum_and_copy(parts, far), "far")
         new = update_rows(
             parts,

time: 105 us -> 101 us (0.962)
  blocking collectives: 90.8 us -> 88.2 us
    all_to_all x5, blocking collectives: 90.8 us -> 85.9 us  [swap(): return lax.all_to_all(array, axes, 0, 0, tiled=True)]
    all_gather x0 -> x1, blocking collectives: none -> 2.28 us  [on_device(): parts = join_cores(own, lax.all_gather(other, 'veh'))]
where the time goes in v4:
time: 101 us
  blocking collectives  88.2 us (87%)
  Pallas kernels  12.2 us (12%)
    all_to_all x5, blocking collectives, swap(): return lax.all_to_all(array, axes, 0, 0, tiled=True)  85.9 us
    pallas_call x1, Pallas kernels, first_pass(): pl.pallas_call(first_kernel, in_specs=[SMEM, ANY, ANY, ANY, ANY], out_spe...  7.86 us
    pallas_call x1, Pallas kernels, second_pass(): pl.pallas_call(second_kernel, in_specs=[VMEM, VMEM, VMEM, VMEM], out_spec...  3.75 us
    all_gather x1, blocking collectives, on_device(): parts = join_cores(own, lax.all_gather(other, 'veh'))  2.28 us

profile of v4, /device:TPU:2, one launch (start us, length us, event | category | flops | bytes accessed | tf_op | source)
XLA Modules:
  0.0 101.2 jit_solution(8993350490061982330)
XLA Ops:
  0.0 0.0 copy-start
  0.0 0.0 copy-start.3
  0.0 0.0 copy-start.4
  0.0 0.0 copy-start.2
  0.0 0.0 copy-start.1
  0.0 7.9 %first_pass.1 = (bf16[8,2048,256]{2,1,0:T(8,128)(2,1)S(1)}, bf16[16,16,128]{2,1,0:T(8,128)(2,1)S(1)}, bf16[8,128,256]{2,1,0:T(8,128)(2,1)S(1)}, s32[32,128]{1,0:T(8,128)S(1)}) custom-call(s32[1]{0:T(128)} %bitcast.half_ref, bf16[2048,128]{1,0:T(8,128)(2,1)} %veh_ref.1, bf16[4096,128]{1,0:T(8,128)(2,1)} %stop_hbm.1, s32[32,128]{1,0:T(8,128)} %bitcast.11, ...), custom_call_target="tpu_custom_call" | custom-call | tf_op jit(solution)/shard_map/first_pass/pallas_call | solution.py:142
  7.9 27.7 %all_to_all.32.in_ref = bf16[16,16,128]{2,1,0:T(8,128)(2,1)S(1)} all-to-all(bf16[16,16,128]{2,1,0:T(8,128)(2,1)S(1)} %get-tuple-element.11), channel_id=1, replica_groups=mesh['y'=4,'x'=4,'far'=8,'pair'=2,'veh'=2] {'far','pair'}, dimensions={0} | all-to-all | bytes 131072 | tf_op jit(solution)/shard_map/all_to_all | solution.py:311
  35.7 14.0 %all_to_all.33.part_ref = bf16[32,16,128]{2,1,0:T(8,128)(2,1)S(1)} all-to-all(bf16[32,16,128]{2,1,0:T(8,128)(2,1)S(1)} %sum_and_copy.2), channel_id=1, replica_groups=mesh['y'=4,'x'=4,'far'=8,'pair'=2,'veh'=2] {'y','x','veh'}, dimensions={0} | all-to-all | bytes 262144 | tf_op jit(solution)/shard_map/all_to_all | solution.py:311
  49.7 3.8 %second_pass.1 = (f32[32,40,128]{2,1,0:T(8,128)S(1)}, bf16[32,40,128]{2,1,0:T(8,128)(2,1)S(1)}) custom-call(bf16[32,16,128]{2,1,0:T(8,128)(2,1)S(1)} %all_to_all.33.part_ref, bf16[8,128,256]{2,1,0:T(8,128)(2,1)S(1)} %get-tuple-element.12.turned_ref, s32[32,128]{1,0:T(8,128)S(1)} %get-tuple-element.13.int_ref, bf16[8,2048,256]{2,1,0:T(8,128)(2,1)S(1)} %get-tuple-element.14.e_ref), custom_call_target="tpu_custom_call" | custom-call | tf_op jit(solution)/shard_map/second_pass/pallas_call | solution.py:235
  53.5 2.3 %all-gather = bf16[64,40,128]{2,1,0:T(8,128)(2,1)S(1)} all-gather(bf16[32,40,128]{2,1,0:T(8,128)(2,1)S(1)} %get-tuple-element.16), channel_id=2, replica_groups=mesh['y'=4,'x'=4,'far'=8,'pair'=2,'veh'=2] {'veh'}, dimensions={0}, use_global_device_ids=true | all-gather | bytes 983040 | tf_op jit(solution)/shard_map/all_gather | solution.py:345
  55.7 0.1 join_cores.1
  55.8 14.0 %all_to_all.34.in_ref = bf16[32,40,128]{2,1,0:T(8,128)(2,1)S(1)} all-to-all(bf16[32,40,128]{2,1,0:T(8,128)(2,1)S(1)} %join_cores.1), channel_id=1, replica_groups=mesh['y'=4,'x'=4,'far'=8,'pair'=2,'veh'=2] {'y','x','pair'}, dimensions={0} | all-to-all | bytes 655360 | tf_op jit(solution)/shard_map/all_to_all | solution.py:311
  69.9 0.1 sum_and_copy.3
  69.9 16.8 %all_to_all.35.part_ref = bf16[8,40,128]{2,1,0:T(8,128)(2,1)S(1)} all-to-all(bf16[8,40,128]{2,1,0:T(8,128)(2,1)S(1)} %sum_and_copy.3), channel_id=1, replica_groups=mesh['y'=4,'x'=4,'far'=8,'pair'=2,'veh'=2] {'far'}, dimensions={0} | all-to-all | bytes 163840 | tf_op jit(solution)/shard_map/all_to_all | solution.py:311
  86.7 0.0 copy-done
  86.7 0.0 copy-done.3
  86.7 0.0 copy-done.4
  86.7 0.0 copy-done.2
  86.7 0.0 copy-done.1
  86.7 0.4 update_rows.1
  87.1 13.4 %all_to_all.36 = bf16[32,32,128]{2,1,0:T(8,128)(2,1)S(1)} all-to-all(bf16[32,32,128]{2,1,0:T(8,128)(2,1)S(1)} %bitcast.8), channel_id=1, replica_groups=mesh['y'=4,'x'=4,'far'=8,'pair'=2,'veh'=2] {'y','x','pair'}, dimensions={0} | all-to-all | bytes 524288 | tf_op jit(solution)/shard_map/all_to_all | solution.py:311
  100.5 0.7 copy.10
  (1 shorter events, 0.0 us)
Async XLA Ops:
  0.0 86.7 %copy-start = (bf16[2048,128]{1,0:T(8,128)(2,1)S(1)}, bf16[2048,128]{1,0:T(8,128)(2,1)}, u32[]{:S(2)}) copy-start(bf16[2048,128]{1,0:T(8,128)(2,1)} %veh_ref.1) | copy-start | bytes 1572868
  0.0 86.7 %copy-start.3 = (bf16[128,128]{1,0:T(8,128)(2,1)S(1)}, bf16[128,128]{1,0:T(8,128)(2,1)}, u32[]{:S(2)}) copy-start(bf16[128,128]{1,0:T(8,128)(2,1)} %projector_ref.1) | copy-start | bytes 98308
  0.0 86.7 %copy-start.4 = (f32[128]{0:T(128)S(1)}, f32[128]{0:T(128)}, u32[]{:S(2)}) copy-start(f32[128]{0:T(128)} %param.14) | copy-start | bytes 1540
  0.0 86.7 %copy-start.2 = (bf16[128,128]{1,0:T(8,128)(2,1)S(1)}, bf16[128,128]{1,0:T(8,128)(2,1)}, u32[]{:S(2)}) copy-start(bf16[128,128]{1,0:T(8,128)(2,1)} %identity_ref.1) | copy-start | bytes 98308
  0.0 86.7 %copy-start.1 = (bf16[128,128]{1,0:T(8,128)(2,1)S(1)}, bf16[128,128]{1,0:T(8,128)(2,1)}, u32[]{:S(2)}) copy-start(bf16[128,128]{1,0:T(8,128)(2,1)} %average_ref.1) | copy-start | bytes 98308

commit v5 on v4

--- a/solution.py
+++ b/solution.py
@@ -11,7 +11,7 @@
 BF16 = jnp.bfloat16
 LANES = 128
 BLOCK = 256
-CHUNK = 256
+CHUNK = 512
 TALL = 512
 LOG2E = 1.4426950408889634
 ROW_BITS = 90.0
@@ -128,8 +128,8 @@
     for k in range(vehicles // LANES):
         rows = pl.ds(k * LANES, LANES)
         col = jnp.zeros((LANES, LANES), F32)
-        for b in range(blocks):
-            t = e_ref[b, rows, :] * share_ref[b]
+        for b in range(0, blocks, 2):
+            t = e_ref[b, rows, :] * share_ref[b] + e_ref[b + 1, rows, :] * share_ref[b + 1]
             t = t[:, 0:LANES] + t[:, LANES:BLOCK]
             col = col + t.astype(F32)
         col = jnp.sum(col.T, axis=0, keepdims=True).astype(out_ref.dtype)
@@ -197,8 +197,8 @@
         for c in range(vehicles // CHUNK):
             rows = pl.ds(c * CHUNK, CHUNK)
             g = jnp.concatenate([g_ref[rows, :]] * (BLOCK // LANES), axis=1)
-            t = (e_ref[b, rows, :] * g).reshape(CHUNK // 32, 2, 16, BLOCK)
-            t = (t[:, 0] + t[:, 1]).astype(F32)
+            t = (e_ref[b, rows, :] * g).reshape(CHUNK // 64, 4, 16, BLOCK)
+            t = ((t[:, 0] + t[:, 1]) + (t[:, 2] + t[:, 3])).astype(F32)
             total = total + jnp.sum(t, axis=0)
         total = jnp.sum(total, axis=0, keepdims=True)
         weight = (loads_of(int_ref, b) * WEIGHT_SCALE / total).astype(BF16)

time: 101 us -> 101 us (level)
  no operation moved by 1% of the time
where the time goes in v5:
time: 101 us
  blocking collectives  88.2 us (87%)
  Pallas kernels  11.5 us (11%)
    all_to_all x5, blocking collectives, swap(): return lax.all_to_all(array, axes, 0, 0, tiled=True)  85.9 us
    pallas_call x1, Pallas kernels, first_pass(): pl.pallas_call(first_kernel, in_specs=[SMEM, ANY, ANY, ANY, ANY], out_spe...  7.5 us
    pallas_call x1, Pallas kernels, second_pass(): pl.pallas_call(second_kernel, in_specs=[VMEM, VMEM, VMEM, VMEM], out_spec...  3.49 us
    all_gather x1, blocking collectives, on_device(): parts = join_cores(own, lax.all_gather(other, 'veh'))  2.28 us

profile of v5, /device:TPU:2, one launch (start us, length us, event | category | flops | bytes accessed | tf_op | source)
XLA Modules:
  0.0 100.6 jit_solution(4720603315251665027)
XLA Ops:
  0.0 0.0 copy-start
  0.0 0.0 copy-start.3
  0.0 0.0 copy-start.4
  0.0 0.0 copy-start.2
  0.0 0.0 copy-start.1
  0.0 7.5 %first_pass.1 = (bf16[8,2048,256]{2,1,0:T(8,128)(2,1)S(1)}, bf16[16,16,128]{2,1,0:T(8,128)(2,1)S(1)}, bf16[8,128,256]{2,1,0:T(8,128)(2,1)S(1)}, s32[32,128]{1,0:T(8,128)S(1)}) custom-call(s32[1]{0:T(128)} %bitcast.half_ref, bf16[2048,128]{1,0:T(8,128)(2,1)} %veh_ref.1, bf16[4096,128]{1,0:T(8,128)(2,1)} %stop_hbm.1, s32[32,128]{1,0:T(8,128)} %bitcast.11, ...), custom_call_target="tpu_custom_call" | custom-call | tf_op jit(solution)/shard_map/first_pass/pallas_call | solution.py:142
  7.5 27.7 %all_to_all.32.in_ref = bf16[16,16,128]{2,1,0:T(8,128)(2,1)S(1)} all-to-all(bf16[16,16,128]{2,1,0:T(8,128)(2,1)S(1)} %get-tuple-element.11), channel_id=1, replica_groups=mesh['y'=4,'x'=4,'far'=8,'pair'=2,'veh'=2] {'far','pair'}, dimensions={0} | all-to-all | bytes 131072 | tf_op jit(solution)/shard_map/all_to_all | solution.py:311
  35.3 14.0 %all_to_all.33.part_ref = bf16[32,16,128]{2,1,0:T(8,128)(2,1)S(1)} all-to-all(bf16[32,16,128]{2,1,0:T(8,128)(2,1)S(1)} %sum_and_copy.2), channel_id=1, replica_groups=mesh['y'=4,'x'=4,'far'=8,'pair'=2,'veh'=2] {'y','x','veh'}, dimensions={0} | all-to-all | bytes 262144 | tf_op jit(solution)/shard_map/all_to_all | solution.py:311
  49.3 3.5 %second_pass.1 = (f32[32,40,128]{2,1,0:T(8,128)S(1)}, bf16[32,40,128]{2,1,0:T(8,128)(2,1)S(1)}) custom-call(bf16[32,16,128]{2,1,0:T(8,128)(2,1)S(1)} %all_to_all.33.part_ref, bf16[8,128,256]{2,1,0:T(8,128)(2,1)S(1)} %get-tuple-element.12.turned_ref, s32[32,128]{1,0:T(8,128)S(1)} %get-tuple-element.13.int_ref, bf16[8,2048,256]{2,1,0:T(8,128)(2,1)S(1)} %get-tuple-element.14.e_ref), custom_call_target="tpu_custom_call" | custom-call | tf_op jit(solution)/shard_map/second_pass/pallas_call | solution.py:235
  52.8 2.3 %all-gather = bf16[64,40,128]{2,1,0:T(8,128)(2,1)S(1)} all-gather(bf16[32,40,128]{2,1,0:T(8,128)(2,1)S(1)} %get-tuple-element.16), channel_id=2, replica_groups=mesh['y'=4,'x'=4,'far'=8,'pair'=2,'veh'=2] {'veh'}, dimensions={0}, use_global_device_ids=true | all-gather | bytes 983040 | tf_op jit(solution)/shard_map/all_gather | solution.py:345
  55.1 0.1 join_cores.1
  55.2 14.0 %all_to_all.34.in_ref = bf16[32,40,128]{2,1,0:T(8,128)(2,1)S(1)} all-to-all(bf16[32,40,128]{2,1,0:T(8,128)(2,1)S(1)} %join_cores.1), channel_id=1, replica_groups=mesh['y'=4,'x'=4,'far'=8,'pair'=2,'veh'=2] {'y','x','pair'}, dimensions={0} | all-to-all | bytes 655360 | tf_op jit(solution)/shard_map/all_to_all | solution.py:311
  69.2 0.1 sum_and_copy.3
  69.3 16.8 %all_to_all.35.part_ref = bf16[8,40,128]{2,1,0:T(8,128)(2,1)S(1)} all-to-all(bf16[8,40,128]{2,1,0:T(8,128)(2,1)S(1)} %sum_and_copy.3), channel_id=1, replica_groups=mesh['y'=4,'x'=4,'far'=8,'pair'=2,'veh'=2] {'far'}, dimensions={0} | all-to-all | bytes 163840 | tf_op jit(solution)/shard_map/all_to_all | solution.py:311
  86.1 0.0 copy-done
  86.1 0.0 copy-done.3
  86.1 0.0 copy-done.4
  86.1 0.0 copy-done.2
  86.1 0.0 copy-done.1
  86.1 0.4 update_rows.1
  86.5 13.4 %all_to_all.36 = bf16[32,32,128]{2,1,0:T(8,128)(2,1)S(1)} all-to-all(bf16[32,32,128]{2,1,0:T(8,128)(2,1)S(1)} %bitcast.8), channel_id=1, replica_groups=mesh['y'=4,'x'=4,'far'=8,'pair'=2,'veh'=2] {'y','x','pair'}, dimensions={0} | all-to-all | bytes 524288 | tf_op jit(solution)/shard_map/all_to_all | solution.py:311
  99.9 0.7 copy.10
  (1 shorter events, 0.0 us)
Async XLA Ops:
  0.0 86.1 %copy-start = (bf16[2048,128]{1,0:T(8,128)(2,1)S(1)}, bf16[2048,128]{1,0:T(8,128)(2,1)}, u32[]{:S(2)}) copy-start(bf16[2048,128]{1,0:T(8,128)(2,1)} %veh_ref.1) | copy-start | bytes 1572868
  0.0 86.1 %copy-start.3 = (bf16[128,128]{1,0:T(8,128)(2,1)S(1)}, bf16[128,128]{1,0:T(8,128)(2,1)}, u32[]{:S(2)}) copy-start(bf16[128,128]{1,0:T(8,128)(2,1)} %projector_ref.1) | copy-start | bytes 98308
  0.0 86.1 %copy-start.4 = (f32[128]{0:T(128)S(1)}, f32[128]{0:T(128)}, u32[]{:S(2)}) copy-start(f32[128]{0:T(128)} %param.14) | copy-start | bytes 1540
  0.0 86.1 %copy-start.2 = (bf16[128,128]{1,0:T(8,128)(2,1)S(1)}, bf16[128,128]{1,0:T(8,128)(2,1)}, u32[]{:S(2)}) copy-start(bf16[128,128]{1,0:T(8,128)(2,1)} %identity_ref.1) | copy-start | bytes 98308
  0.0 86.1 %copy-start.1 = (bf16[128,128]{1,0:T(8,128)(2,1)S(1)}, bf16[128,128]{1,0:T(8,128)(2,1)}, u32[]{:S(2)}) copy-start(bf16[128,128]{1,0:T(8,128)(2,1)} %average_ref.1) | copy-start | bytes 98308

commit v6 on v5

--- a/solution.py
+++ b/solution.py
@@ -197,8 +197,9 @@
         for c in range(vehicles // CHUNK):
             rows = pl.ds(c * CHUNK, CHUNK)
             g = jnp.concatenate([g_ref[rows, :]] * (BLOCK // LANES), axis=1)
-            t = (e_ref[b, rows, :] * g).reshape(CHUNK // 64, 4, 16, BLOCK)
-            t = ((t[:, 0] + t[:, 1]) + (t[:, 2] + t[:, 3])).astype(F32)
+            t = (e_ref[b, rows, :] * g).reshape(CHUNK // 128, 8, 16, BLOCK)
+            t = [t[:, 2 * i] + t[:, 2 * i + 1] for i in range(4)]
+            t = ((t[0] + t[1]) + (t[2] + t[3])).astype(F32)
             total = total + jnp.sum(t, axis=0)
         total = jnp.sum(total, axis=0, keepdims=True)
         weight = (loads_of(int_ref, b) * WEIGHT_SCALE / total).astype(BF16)

time: 101 us -> 101 us (level)
  no operation moved by 1% of the time
where the time goes in v6:
time: 101 us; the launch traced here: 100 us
  blocking collectives  88.2 us (87%)
  Pallas kernels  11.4 us (11%)
    all_to_all x5, blocking collectives, swap(): return lax.all_to_all(array, axes, 0, 0, tiled=True)  85.9 us
    pallas_call x1, Pallas kernels, first_pass(): pl.pallas_call(first_kernel, in_specs=[SMEM, ANY, ANY, ANY, ANY], out_spe...  7.5 us
    pallas_call x1, Pallas kernels, second_pass(): pl.pallas_call(second_kernel, in_specs=[VMEM, VMEM, VMEM, VMEM], out_spec...  3.37 us
    all_gather x1, blocking collectives, on_device(): parts = join_cores(own, lax.all_gather(other, 'veh'))  2.28 us

profile of v6, /device:TPU:2, one launch (start us, length us, event | category | flops | bytes accessed | tf_op | source)
XLA Modules:
  0.0 100.4 jit_solution(579870506337364012)
XLA Ops:
  0.0 0.0 copy-start
  0.0 0.0 copy-start.3
  0.0 0.0 copy-start.4
  0.0 0.0 copy-start.2
  0.0 0.0 copy-start.1
  0.0 7.5 %first_pass.1 = (bf16[8,2048,256]{2,1,0:T(8,128)(2,1)S(1)}, bf16[16,16,128]{2,1,0:T(8,128)(2,1)S(1)}, bf16[8,128,256]{2,1,0:T(8,128)(2,1)S(1)}, s32[32,128]{1,0:T(8,128)S(1)}) custom-call(s32[1]{0:T(128)} %bitcast.half_ref, bf16[2048,128]{1,0:T(8,128)(2,1)} %veh_ref.1, bf16[4096,128]{1,0:T(8,128)(2,1)} %stop_hbm.1, s32[32,128]{1,0:T(8,128)} %bitcast.11, ...), custom_call_target="tpu_custom_call" | custom-call | tf_op jit(solution)/shard_map/first_pass/pallas_call | solution.py:142
  7.5 27.7 %all_to_all.32.in_ref = bf16[16,16,128]{2,1,0:T(8,128)(2,1)S(1)} all-to-all(bf16[16,16,128]{2,1,0:T(8,128)(2,1)S(1)} %get-tuple-element.11), channel_id=1, replica_groups=mesh['y'=4,'x'=4,'far'=8,'pair'=2,'veh'=2] {'far','pair'}, dimensions={0} | all-to-all | bytes 131072 | tf_op jit(solution)/shard_map/all_to_all | solution.py:312
  35.3 14.0 %all_to_all.33.part_ref = bf16[32,16,128]{2,1,0:T(8,128)(2,1)S(1)} all-to-all(bf16[32,16,128]{2,1,0:T(8,128)(2,1)S(1)} %sum_and_copy.2), channel_id=1, replica_groups=mesh['y'=4,'x'=4,'far'=8,'pair'=2,'veh'=2] {'y','x','veh'}, dimensions={0} | all-to-all | bytes 262144 | tf_op jit(solution)/shard_map/all_to_all | solution.py:312
  49.3 3.4 %second_pass.1 = (f32[32,40,128]{2,1,0:T(8,128)S(1)}, bf16[32,40,128]{2,1,0:T(8,128)(2,1)S(1)}) custom-call(bf16[32,16,128]{2,1,0:T(8,128)(2,1)S(1)} %all_to_all.33.part_ref, bf16[8,128,256]{2,1,0:T(8,128)(2,1)S(1)} %get-tuple-element.12.turned_ref, s32[32,128]{1,0:T(8,128)S(1)} %get-tuple-element.13.int_ref, bf16[8,2048,256]{2,1,0:T(8,128)(2,1)S(1)} %get-tuple-element.14.e_ref), custom_call_target="tpu_custom_call" | custom-call | tf_op jit(solution)/shard_map/second_pass/pallas_call | solution.py:236
  52.7 2.3 %all-gather = bf16[64,40,128]{2,1,0:T(8,128)(2,1)S(1)} all-gather(bf16[32,40,128]{2,1,0:T(8,128)(2,1)S(1)} %get-tuple-element.16), channel_id=2, replica_groups=mesh['y'=4,'x'=4,'far'=8,'pair'=2,'veh'=2] {'veh'}, dimensions={0}, use_global_device_ids=true | all-gather | bytes 983040 | tf_op jit(solution)/shard_map/all_gather | solution.py:346
  55.0 0.1 join_cores.1
  55.1 14.0 %all_to_all.34.in_ref = bf16[32,40,128]{2,1,0:T(8,128)(2,1)S(1)} all-to-all(bf16[32,40,128]{2,1,0:T(8,128)(2,1)S(1)} %join_cores.1), channel_id=1, replica_groups=mesh['y'=4,'x'=4,'far'=8,'pair'=2,'veh'=2] {'y','x','pair'}, dimensions={0} | all-to-all | bytes 655360 | tf_op jit(solution)/shard_map/all_to_all | solution.py:312
  69.1 0.1 sum_and_copy.3
  69.2 16.8 %all_to_all.35.part_ref = bf16[8,40,128]{2,1,0:T(8,128)(2,1)S(1)} all-to-all(bf16[8,40,128]{2,1,0:T(8,128)(2,1)S(1)} %sum_and_copy.3), channel_id=1, replica_groups=mesh['y'=4,'x'=4,'far'=8,'pair'=2,'veh'=2] {'far'}, dimensions={0} | all-to-all | bytes 163840 | tf_op jit(solution)/shard_map/all_to_all | solution.py:312
  86.0 0.0 copy-done
  86.0 0.0 copy-done.3
  86.0 0.0 copy-done.4
  86.0 0.0 copy-done.2
  86.0 0.0 copy-done.1
  86.0 0.4 update_rows.1
  86.4 13.4 %all_to_all.36 = bf16[32,32,128]{2,1,0:T(8,128)(2,1)S(1)} all-to-all(bf16[32,32,128]{2,1,0:T(8,128)(2,1)S(1)} %bitcast.8), channel_id=1, replica_groups=mesh['y'=4,'x'=4,'far'=8,'pair'=2,'veh'=2] {'y','x','pair'}, dimensions={0} | all-to-all | bytes 524288 | tf_op jit(solution)/shard_map/all_to_all | solution.py:312
  99.7 0.7 copy.10
  (1 shorter events, 0.0 us)
Async XLA Ops:
  0.0 86.0 %copy-start = (bf16[2048,128]{1,0:T(8,128)(2,1)S(1)}, bf16[2048,128]{1,0:T(8,128)(2,1)}, u32[]{:S(2)}) copy-start(bf16[2048,128]{1,0:T(8,128)(2,1)} %veh_ref.1) | copy-start | bytes 1572868
  0.0 86.0 %copy-start.3 = (bf16[128,128]{1,0:T(8,128)(2,1)S(1)}, bf16[128,128]{1,0:T(8,128)(2,1)}, u32[]{:S(2)}) copy-start(bf16[128,128]{1,0:T(8,128)(2,1)} %projector_ref.1) | copy-start | bytes 98308
  0.0 86.0 %copy-start.4 = (f32[128]{0:T(128)S(1)}, f32[128]{0:T(128)}, u32[]{:S(2)}) copy-start(f32[128]{0:T(128)} %param.14) | copy-start | bytes 1540
  0.0 86.0 %copy-start.2 = (bf16[128,128]{1,0:T(8,128)(2,1)S(1)}, bf16[128,128]{1,0:T(8,128)(2,1)}, u32[]{:S(2)}) copy-start(bf16[128,128]{1,0:T(8,128)(2,1)} %identity_ref.1) | copy-start | bytes 98308
  0.0 86.0 %copy-start.1 = (bf16[128,128]{1,0:T(8,128)(2,1)S(1)}, bf16[128,128]{1,0:T(8,128)(2,1)}, u32[]{:S(2)}) copy-start(bf16[128,128]{1,0:T(8,128)(2,1)} %average_ref.1) | copy-start | bytes 98308
